TPU v7x, 512 devices: a whole 4x4x16 slice. The times are simulated.
512 devices in a mesh: dom: 128 (over x, z, core), rep: 4 (over y).
Axes of the slice: x: 4, y: 4, z: 16, core: 2. Of those that a mesh axis runs over, the one named last changes fastest.
Arguments:
- feats: bfloat16 [524288, 256], P(('dom', 'rep')), may hold values from -6 to 6
- w_self: bfloat16 [256, 256], replicated, may hold values from -0.375 to 0.375
- w_neigh: bfloat16 [256, 256], replicated, may hold values from -0.375 to 0.375
- bias: float32 [256], replicated, may hold values from -3 to 3
- out_cot: bfloat16 [524288, 256], P(('dom', 'rep')), may hold values from -6 to 6
- degree: int32 [524288], P(('dom', 'rep')), may hold values from 1 to 20
- edge_src: int32 [524288, 10], P(('dom', 'rep')), may hold values from 0 to 2559, as said below
- hub_rows: int32 [1024], P(('dom', 'rep')), may hold values from 0 to 1023, as said below
- send_rows: int32 [65536, 4], P(('dom', 'rep')), may hold values from -1 to 1023, as said below
Outputs:
- outputs: bfloat16 [524288, 256], P(('dom', 'rep'))
- grad_feats: bfloat16 [524288, 256], P(('dom', 'rep'))
- unit_w_self: float32 [256, 256], replicated
- unit_w_neigh: float32 [256, 256], replicated
- unit_bias: float32 [256], replicated
Inputs may be any that keep to these rules, and one draw needn't show every extreme that they name: `hub_rows`: the 2 entries of one block are distinct rows of that block. `send_rows`: row q * 128 + e lists rows of block q for partition e: live entries first, then -1; every list has a live entry, every block has a full list, and one partition receives full lists from all blocks. `edge_src`: A slot of the halo part of a block's table always names a live entry of the list it comes from.
All inputs are finite; a program needn't handle non-finite values.
Results may differ from a plain program's by a relative error of at most 0.0056.
Values may be sent and summed in bfloat16 or wider, within the bound.
A program may use at most 128 MiB of HBM per device.

v0:
```python
import jax
import jax.numpy as jnp
from jax import lax
from jax.sharding import PartitionSpec as P

NORM_EPS = 1e-05
UNIT_EPS = 1e-06


def output_head(preact):
    act = jax.nn.elu(preact)
    return act * lax.rsqrt(jnp.mean(act * act, axis=-1, keepdims=True) + NORM_EPS)


def unit_scale(grad):
    return grad * lax.rsqrt(jnp.mean(grad * grad) + UNIT_EPS)


def on_device(feats, w_self, w_neigh, bias, out_cot, degree, edge_src, hub_rows, send_rows):
    block_rows, feat_width = feats.shape
    fanout = edge_src.shape[1]
    zero_half = jnp.zeros((), jnp.bfloat16)
    hub_own = feats[hub_rows]
    hub_table = lax.all_gather(hub_own, ("dom", "rep"), axis=0, tiled=True)
    listed = send_rows >= 0
    send_safe = jnp.maximum(send_rows, 0)
    outgoing = jnp.where(listed[:, :, None], feats[send_safe], zero_half)
    incoming = lax.all_to_all(outgoing, "dom", split_axis=0, concat_axis=0, tiled=True)
    hub_count = hub_table.shape[0]
    halo_count = incoming.shape[0] * incoming.shape[1]
    slot_table = jnp.concatenate(
        [feats, hub_table, incoming.reshape(halo_count, feat_width)], axis=0
    )
    valid_count = jnp.minimum(degree, fanout)
    live_mask = jnp.arange(fanout, dtype=jnp.int32)[None, :] < valid_count[:, None]
    gathered = jnp.where(live_mask[:, :, None], slot_table[edge_src], zero_half)
    summed = jnp.sum(gathered, axis=1, dtype=jnp.float32)
    divisor = valid_count.astype(jnp.float32)[:, None]
    neighbor_mean = (summed / divisor).astype(jnp.bfloat16)
    preact = (
        jnp.dot(feats, w_self, preferred_element_type=jnp.float32)
        + jnp.dot(neighbor_mean, w_neigh, preferred_element_type=jnp.float32)
        + bias
    )
    outputs, backward = jax.vjp(output_head, preact)
    (grad_pre,) = backward(out_cot.astype(jnp.float32))
    grad_low = grad_pre.astype(jnp.bfloat16)
    row_contract = (((0,), (0,)), ((), ()))
    col_contract = (((1,), (1,)), ((), ()))
    wself_part = lax.dot_general(feats, grad_low, row_contract, preferred_element_type=jnp.float32)
    wneigh_part = lax.dot_general(
        neighbor_mean, grad_low, row_contract, preferred_element_type=jnp.float32
    )
    bias_part = jnp.sum(grad_pre, axis=0)
    feat_grad = lax.dot_general(grad_low, w_self, col_contract, preferred_element_type=jnp.float32)
    edge_grad = (
        lax.dot_general(grad_low, w_neigh, col_contract, preferred_element_type=jnp.float32)
        / divisor
    )
    edge_terms = jnp.where(live_mask[:, :, None], edge_grad[:, None, :], jnp.float32(0.0)).reshape(
        -1, feat_width
    )
    slot_grad = (
        jnp.zeros((slot_table.shape[0], feat_width), jnp.float32)
        .at[edge_src.reshape(-1)]
        .add(edge_terms)
    )
    hub_grad = slot_grad[block_rows : block_rows + hub_count]
    halo_grad = slot_grad[block_rows + hub_count :].reshape(
        incoming.shape[0], incoming.shape[1], feat_width
    )
    returned = lax.all_to_all(
        halo_grad.astype(jnp.bfloat16), "dom", split_axis=0, concat_axis=0, tiled=True
    ).astype(halo_grad.dtype)
    feat_grad = feat_grad + slot_grad[:block_rows]
    feat_grad = feat_grad.at[send_safe.reshape(-1)].add(
        jnp.where(listed[:, :, None], returned, jnp.float32(0.0)).reshape(-1, feat_width)
    )
    wself_sum, wneigh_sum, bias_sum = lax.psum((wself_part, wneigh_part, bias_part), ("dom", "rep"))
    hub_mine = lax.psum_scatter(hub_grad, ("dom", "rep"), scatter_dimension=0, tiled=True)
    feat_grad = feat_grad.at[hub_rows].add(hub_mine)
    return (
        outputs.astype(jnp.bfloat16),
        feat_grad.astype(jnp.bfloat16),
        unit_scale(wself_sum),
        unit_scale(wneigh_sum),
        unit_scale(bias_sum),
    )


def solution(mesh):
    placed = (
        P(("dom", "rep"), None),
        P(),
        P(),
        P(),
        P(("dom", "rep"), None),
        P(("dom", "rep")),
        P(("dom", "rep"), None),
        P(("dom", "rep")),
        P(("dom", "rep"), None),
    )
    return jax.shard_map(
        on_device,
        mesh=mesh,
        in_specs=placed,
        out_specs=(P(("dom", "rep"), None), P(("dom", "rep"), None), P(), P(), P()),
        check_vma=False,
    )
```

profile of v0, /device:TPU:1, one launch (start us, length us, event | category | flops | bytes accessed | tf_op | source)
XLA Modules:
  0.0 900.0 jit_solution(17739084312274609060)
XLA Ops:
  8.9 2.7 gather_fusion.1
  12.8 20.4 %all-to-all-start = ((bf16[128,4,256]{2,1,0:T(4,128)(2,1)}), bf16[128,4,256]{2,1,0:T(4,128)(2,1)S(1)}, u32[]{:S(2)}, u32[]{:S(2)}) async-start(bf16[128,4,256]{2,1,0:T(4,128)(2,1)} %broadcast_select_fusion), calls=%async_computation | async-start | bytes 524288 | tf_op jit(solution)/shard_map/all_to_all | solution.py:28
  34.1 197.5 %all-gather.1 = bf16[512,2,256]{2,1,0:T(2,128)(2,1)S(1)} all-gather(bf16[1,2,256]{2,1,0:T(2,128)(2,1)S(1)} %bitcast.19), channel_id=2, replica_groups=mesh['dom'=128,'rep'=4] {'dom','rep'}, dimensions={0}, use_global_device_ids=true | all-gather | bytes 525312 | tf_op jit(solution)/shard_map/all_gather | solution.py:24
  233.0 1.2 copy.29
  234.9 1.3 fusion.13
  236.4 41.1 %gather_fusion.2 = bf16[10240,256]{1,0:T(8,128)(2,1)} fusion(bf16[2560,256]{1,0:T(8,128)(2,1)S(1)} %pad_maximum_fusion, s32[10240]{0:T(1024)S(1)} %broadcast_clamp_fusion), kind=kCustom, calls=%fused_computation.2 | custom fusion | bytes 10526720 | tf_op jit(solution)/shard_map/gather | solution.py:36
  277.5 10.5 %reshape.149 = bf16[1024,10,256]{2,1,0:T(8,128)(2,1)} reshape(bf16[10240,256]{1,0:T(8,128)(2,1)} %gather_fusion.2) | data formatting | bytes 10485760 | tf_op jit(solution)/shard_map/gather | solution.py:36
  287.9 23.5 %convert_reduce_fusion = f32[1024,256]{1,0:T(8,128)S(1)} fusion(bf16[1024,10,256]{2,1,0:T(8,128)(2,1)} %reshape.149, pred[1024,10]{1,0:T(8,128)(4,1)S(1)} %iota_compare_fusion), kind=kLoop, calls=%fused_computation.6 | loop fusion | flops 7602176 | bytes 6301696 | tf_op jit(solution)/shard_map/reduce_sum | solution.py:37
  312.6 2.2 fusion.12
  317.3 7.1 broadcast_in_dim.103
  324.4 14.8 %broadcast_in_dim.104 = f32[10240,256]{1,0:T(8,128)} reshape(f32[1024,10,256]{2,1,0:T(8,128)} %broadcast_in_dim.103) | data formatting | bytes 20971520 | tf_op jit(solution)/shard_map/jit(_where)/broadcast_in_dim | solution.py:60
  339.2 62.1 %scatter_custom_fusion = f32[2560,256]{1,0:T(8,128)S(1)} fusion(s32[10240]{0:T(1024)S(1)} %bitcast.17, f32[10240,256]{1,0:T(8,128)} %broadcast_in_dim.104, f32[]{:T(128)} %constant.17.clone.1, pred[10240]{0:T(1024)(128)(4,1)S(1)} %lt.66), kind=kCustom, calls=%fused_computation.7 | custom fusion | flops 5242880 | bytes 13118464 | tf_op jit(solution)/shard_map/scatter-add | solution.py:66
  403.9 16.6 %all-to-all-start.1 = ((bf16[128,4,256]{2,1,0:T(4,128)(2,1)}), bf16[128,4,256]{2,1,0:T(4,128)(2,1)S(1)}, u32[]{:S(2)}, u32[]{:S(2)}) async-start(bf16[128,4,256]{2,1,0:T(4,128)(2,1)} %convert_element_type.34), calls=%async_computation.1 | async-start | bytes 524288 | tf_op jit(solution)/shard_map/all_to_all | solution.py:72
  420.5 105.4 %psum.23 = f32[256]{0:T(256)} all-reduce(f32[256]{0:T(256)} %get-tuple-element.25), channel_id=1, replica_groups=mesh['dom'=128,'rep'=4] {'dom','rep'}, use_global_device_ids=true, to_apply=%region_12.13 | all-reduce | flops 256 | bytes 2048 | tf_op jit(solution)/shard_map/psum | solution.py:79
  525.9 1.3 multiply_reduce_fusion.3
  527.8 1.2 broadcast_multiply_fusion.2
  529.1 2.0 copy.32
  531.1 1.7 convolution_add_fusion
  532.8 346.0 %all-reduce.4.cloned.1.call-done = (f32[1024,256]{1,0:T(8,128)}, f32[256,256]{0,1:T(8,128)}, f32[256,256]{1,0:T(8,128)}) async-done(((f32[1024,256]{1,0:T(8,128)}, f32[256,256]{0,1:T(8,128)}, f32[256,256]{1,0:T(8,128)}), (f32[1024,256]{1,0:T(8,128)}, f32[256,256]{0,1:T(8,128)}, f32[256,256]{1,0:T(8,128)})) %all-reduce.4.cloned.1.call-update) | async-done | bytes 1572880
  878.8 1.6 multiply_reduce_fusion.1
  881.1 1.6 multiply_reduce_fusion.2
  885.3 1.7 broadcast_multiply_fusion
  887.3 3.7 scatter_fusion
  891.1 1.2 scatter_custom_fusion.2
  (66 shorter events, 14.9 us)
Async XLA Ops:
  7.2 304.5 %copy-start = (bf16[256,256]{1,0:T(8,128)(2,1)S(1)}, bf16[256,256]{1,0:T(8,128)(2,1)}, u32[]{:S(2)}) copy-start(bf16[256,256]{1,0:T(8,128)(2,1)} %param.11) | copy-start | bytes 393220
  7.2 26.3 %copy-start.1 = (bf16[1024,256]{1,0:T(8,128)(2,1)S(1)}, bf16[1024,256]{1,0:T(8,128)(2,1)}, u32[]{:S(2)}) copy-start(bf16[1024,256]{1,0:T(8,128)(2,1)} %param.9) | copy-start | bytes 1572868
  7.2 26.0 %copy-start.5 = (s32[1024,10]{0,1:T(8,128)S(1)}, s32[1024,10]{0,1:T(8,128)}, u32[]{:S(2)}) copy-start(s32[1024,10]{0,1:T(8,128)} %param.15) | copy-start | bytes 122884
  7.2 26.3 %copy-start.10 = (s32[2]{0:T(128)S(1)}, s32[2]{0:T(128)}, u32[]{:S(2)}) copy-start(s32[2]{0:T(128)} %param.16) | copy-start | bytes 28
  7.2 224.8 %copy-start.7 = (s32[1024]{0:T(1024)S(1)}, s32[1024]{0:T(1024)}, u32[]{:S(2)}) copy-start(s32[1024]{0:T(1024)} %param.14) | copy-start | bytes 12292
  8.9 226.0 %copy-start.4 = (bf16[256,256]{1,0:T(8,128)(2,1)S(1)}, bf16[256,256]{1,0:T(8,128)(2,1)}, u32[]{:S(2)}) copy-start(bf16[256,256]{1,0:T(8,128)(2,1)} %param.10) | copy-start | bytes 393220
  12.8 223.5 %all-to-all-start = ((bf16[128,4,256]{2,1,0:T(4,128)(2,1)}), bf16[128,4,256]{2,1,0:T(4,128)(2,1)S(1)}, u32[]{:S(2)}, u32[]{:S(2)}) async-start(bf16[128,4,256]{2,1,0:T(4,128)(2,1)} %broadcast_select_fusion), calls=%async_computation | async-start | bytes 524288 | tf_op jit(solution)/shard_map/all_to_all | solution.py:28
  33.2 845.6 %all-reduce.4.cloned.1.call-start = ((), (), s32[]{:S(2)}) async-start(), calls=%async_computation.2 | async-start | bytes 3145728
  33.5 198.6 %copy-start.8 = (s32[2]{0:T(128)}, s32[2]{0:T(128)S(1)}, u32[]{:S(2)}) copy-start(s32[2]{0:T(128)S(1)} %compare_select_fusion.5) | copy-start | bytes 28
  287.9 23.8 %copy-start.3 = (f32[1024,256]{0,1:T(8,128)S(1)}, f32[1024,256]{0,1:T(8,128)}, u32[]{:S(2)}) copy-start(f32[1024,256]{0,1:T(8,128)} %fusion.13) | copy-start | bytes 3145732
  287.9 23.8 %copy-start.9 = (f32[256]{0:T(256)S(1)}, f32[256]{0:T(256)}, u32[]{:S(2)}) copy-start(f32[256]{0:T(256)} %param.12) | copy-start | bytes 3076
  401.3 127.8 %copy-start.2 = (f32[2560,256]{1,0:T(8,128)}, f32[2560,256]{1,0:T(8,128)S(1)}, u32[]{:S(2)}) copy-start(f32[2560,256]{1,0:T(8,128)S(1)} %scatter_custom_fusion) | copy-start | bytes 7864324
  403.9 483.0 %all-to-all-start.1 = ((bf16[128,4,256]{2,1,0:T(4,128)(2,1)}), bf16[128,4,256]{2,1,0:T(4,128)(2,1)S(1)}, u32[]{:S(2)}, u32[]{:S(2)}) async-start(bf16[128,4,256]{2,1,0:T(4,128)(2,1)} %convert_element_type.34), calls=%async_computation.1 | async-start | bytes 524288 | tf_op jit(solution)/shard_map/all_to_all | solution.py:72
  531.1 356.2 %copy-start.6 = (s32[512,1]{0,1:T(1,128)S(1)}, s32[512,1]{0,1:T(1,128)}, u32[]{:S(2)}) copy-start(s32[512,1]{0,1:T(1,128)} %compare_select_fusion.4) | copy-start | bytes 6148
Sparse Core Ops, SparseCore 0:
  402.6 476.1 all-reduce.3
where the time goes:
time: 902 us; the launch traced here: 900 us
  waiting for transfers between devices  346 us (38%)
  blocking collectives  303 us (34%)
  other arithmetic  106 us (12%)
  local copies, waits for them, and re-layouts  85.4 us (9%)
  starting transfers between devices  37 us (4%)
  between operations  16.5 us (2%)
    unnamed x2, waiting for transfers between devices  346 us
    all_gather x1, blocking collectives, on_device(): hub_table = lax.all_gather(hub_own, ('dom', 'rep'), axis=0, tiled=True)  198 us
    psum x1, blocking collectives, on_device(): lax.psum((wself_part, wneigh_part, bias_part), ('dom', 'rep'))  105 us
    scatter-add x1, other arithmetic, on_device(): slot_grad = jnp.zeros((slot_table.shape[0], feat_width), jnp.float32).at[...  62.1 us
    gather x2, local copies, waits for them, and re-layouts, on_device(): gathered = jnp.where(live_mask[:, :, None], slot_table[edge_src], zero_half)  51.5 us
    reduce_sum x1, other arithmetic, on_device(): summed = jnp.sum(gathered, axis=1, dtype=jnp.float32)  23.5 us
    broadcast_in_dim x2, local copies, waits for them, and re-layouts, on_device(): jnp.where(live_mask[:, :, None], edge_grad[:, None, :], jnp.float32(0.0))  21.9 us
    all_to_all x1, starting transfers between devices, on_device(): lax.all_to_all(outgoing, 'dom', split_axis=0, concat_axis=0, tiled=True)  20.4 us
  transfers between devices with their start and end apart: 3, of which 1 were waited for; matrix products, arithmetic and copies ran while one was open for 2% of the time, Pallas kernels for 0%

commit v1 on v0

v1 whole, which is shorter than its diff:
```python
import jax
import jax.numpy as jnp
from jax import lax
from jax.experimental import pallas as pl
from jax.experimental.pallas import tpu as pltpu
from jax.sharding import PartitionSpec as P

NORM_EPS = 1e-05
UNIT_EPS = 1e-06
NX, NZ, NC, NY = 4, 16, 2, 4
NYX = NY * NX
NXC = NX * NC
MESH = pl.DeviceIdType.MESH
F32 = jnp.float32
BF16 = jnp.bfloat16


def coords():
    d = lax.axis_index("dom")
    y = lax.axis_index("rep")
    return d // (NZ * NC), (d // NC) % NZ, d % NC, y


def dev(x, z, c, y):
    return ((x * NZ + z) * NC + c, y)


def z_peers(x, z, c, y):
    return [dev(x, (z + i) % NZ, c, y) for i in range(1, NZ)]


def yx_peers(x, z, c, y):
    return [dev((x + i % NX) % NX, z, c, (y + i // NX) % NY) for i in range(1, NYX)]


def xc_peers(x, z, c, y):
    return [dev((x + i // NC) % NX, z, (c + i % NC) % NC, y) for i in range(1, NXC)]


def entry_barrier_signal(x, z, c, y):
    peers = z_peers(x, z, c, y) + xc_peers(x, z, c, y)
    peers += [p for i, p in enumerate(yx_peers(x, z, c, y), 1) if i // NX != 0]
    barrier = pltpu.get_barrier_semaphore()
    for p in peers:
        pl.semaphore_signal(barrier, inc=1, device_id=p, device_id_type=MESH)
    return barrier, len(peers)


def rcopy(src, dst, ssem, rsem, peer):
    return pltpu.make_async_remote_copy(
        src_ref=src, dst_ref=dst, send_sem=ssem, recv_sem=rsem, device_id=peer, device_id_type=MESH
    )


def pick_kernel(feats_ref, send_ref, hub_ref, out_ref, hub_out_ref):
    rows = feats_ref.shape[0]
    feats = feats_ref[...]
    idx = send_ref[...]
    lane = lax.broadcasted_iota(jnp.int32, (idx.shape[0], rows), 1)
    hot = jnp.where(idx == lane, 1.0, 0.0).astype(BF16)
    out_ref[...] = jnp.dot(hot, feats, preferred_element_type=F32).astype(BF16)
    hidx = hub_ref[...]
    hlane = lax.broadcasted_iota(jnp.int32, (8, rows), 1)
    hhot = jnp.where(hidx == hlane, 1.0, 0.0).astype(BF16)
    hub_out_ref[...] = jnp.dot(hhot, feats, preferred_element_type=F32)[:2]


def fwd_exchange_kernel(s_ref, hub_ref, edge_ref, deg_ref, h_ref, hubtab_ref, a_ref,
                        t_ref, zbuf, z32, eslot,
                        own_sem, x_ss, x_rs, z_ss, z_rs, hz_ss, hz_rs, hp_ss, hp_rs, hc_ss, hc_rs):
    x, z, c, y = coords()
    xc = x * NC + c
    yx = y * NX + x
    barrier, nbar = entry_barrier_signal(x, z, c, y)
    rows, fan = edge_ref.shape
    slots = a_ref.shape[1]
    hubs = 2 * NC * NYX * NZ

    e = edge_ref[...]
    h = e - rows
    hub_pos = ((((h // (2 * NY)) % NC * NY + (h // 2) % NY) * NX + h // (2 * NY * NC * NZ)) * NZ
               + (h // (2 * NY * NC)) % NZ) * 2 + h % 2
    g = h - hubs
    halo_pos = (((g // (4 * NC)) % NZ * NX + g // (4 * NC * NZ)) * NC + (g // 4) % NC) * 4 + g % 4
    pos = jnp.where(e < rows, e, jnp.where(e < rows + hubs, rows + hub_pos, rows + hubs + halo_pos))
    live = lax.broadcasted_iota(jnp.int32, e.shape, 1) < jnp.minimum(deg_ref[...], fan)
    eslot[...] = jnp.where(live, pos, -1)

    step = 16
    tile = min(128, slots)

    def build(lo, hi):
        def body(b, carry):
            r0 = pl.multiple_of(b * step, step)
            ids = eslot[pl.ds(r0, step), :]
            lane = lax.broadcasted_iota(jnp.int32, (step, tile), 1)
            diff = [ids[:, k:k + 1] - lane for k in range(fan)]
            for t in range(slots // tile):
                acc = jnp.zeros((step, tile), F32)
                for k in range(fan):
                    acc = acc + jnp.where(diff[k] == t * tile, 1.0, 0.0)
                a_ref[pl.ds(r0, step), t * tile:(t + 1) * tile] = acc.astype(BF16)
            return carry
        lax.fori_loop(lo, hi, body, 0)

    nblk = rows // step
    cuts = [0, nblk // 8, nblk * 3 // 8, nblk * 6 // 8, nblk]

    own = [pltpu.make_async_copy(s_ref.at[xc], t_ref.at[:, xc], own_sem.at[0]),
           pltpu.make_async_copy(hub_ref, zbuf.at[z], own_sem.at[1])]
    for cp in own:
        cp.start()
    build(cuts[0], cuts[1])
    pl.semaphore_wait(barrier, nbar)

    hz = [rcopy(hub_ref, zbuf.at[z], hz_ss.at[i], hz_rs.at[i], p)
          for i, p in enumerate(z_peers(x, z, c, y))]
    for cp in hz:
        cp.start()
    st1 = []
    for i, p in enumerate(xc_peers(x, z, c, y), 1):
        pxc = ((x + i // NC) % NX) * NC + (c + i % NC) % NC
        st1.append(rcopy(s_ref.at[pxc], t_ref.at[:, xc], x_ss.at[i - 1], x_rs.at[i - 1], p))
    for cp in st1:
        cp.start()
    build(cuts[1], cuts[2])
    for cp in own:
        cp.wait()
    for cp in st1:
        cp.wait_recv()
    own2 = pltpu.make_async_copy(t_ref.at[z], h_ref.at[z], own_sem.at[2])
    own2.start()
    st2 = [rcopy(t_ref.at[(z + i) % NZ], h_ref.at[z], z_ss.at[i - 1], z_rs.at[i - 1], p)
           for i, p in enumerate(z_peers(x, z, c, y), 1)]
    for cp in st2:
        cp.start()
    for cp in hz:
        cp.wait_recv()
    for i in range(NZ):
        z32[2 * i:2 * i + 2, :] = zbuf[i]
    hubtab_ref[c, yx] = z32[...].astype(BF16)
    hp = [rcopy(hubtab_ref.at[c, yx], hubtab_ref.at[c, yx], hp_ss.at[i], hp_rs.at[i], p)
          for i, p in enumerate(yx_peers(x, z, c, y))]
    for cp in hp:
        cp.start()
    build(cuts[2], cuts[3])
    for cp in hp:
        cp.wait_recv()
    hc = rcopy(hubtab_ref.at[c], hubtab_ref.at[c], hc_ss, hc_rs, dev(x, z, 1 - c, y))
    hc.start()
    build(cuts[3], cuts[4])
    hc.wait_recv()
    own2.wait()
    for cp in st2:
        cp.wait_recv()
    for cp in hz + st1 + st2 + hp + [hc]:
        cp.wait_send()


def layer_kernel(feats_ref, hub_ref, halo_ref, a_ref, ws_ref, wn_ref, bias_ref, cot_ref, deg_ref,
                 out_ref, base_ref, hubg_ref, halog_ref, wg_ref, bg_ref, nm_ref, gl_ref, eg_ref):
    rows, width = feats_ref.shape
    nh = hub_ref.shape[0]
    ng = halo_ref.shape[0]
    fan = 10
    nt = (((1,), (1,)), ((), ()))
    tn = (((0,), (0,)), ((), ()))
    blk = min(256, rows)
    bsum = jnp.zeros((1, width), F32)
    for b in range(rows // blk):
        rs = slice(b * blk, (b + 1) * blk)
        summed = jnp.dot(a_ref[rs, :rows], feats_ref[...], preferred_element_type=F32)
        summed += jnp.dot(a_ref[rs, rows:rows + nh], hub_ref[...], preferred_element_type=F32)
        summed += jnp.dot(a_ref[rs, rows + nh:], halo_ref[...], preferred_element_type=F32)
        divisor = jnp.minimum(deg_ref[rs, :], fan).astype(F32)
        nm = (summed / divisor).astype(BF16)
        nm_ref[rs, :] = nm
        pre = (jnp.dot(feats_ref[rs, :], ws_ref[...], preferred_element_type=F32)
               + jnp.dot(nm, wn_ref[...], preferred_element_type=F32) + bias_ref[...])
        ex = jnp.exp(jnp.minimum(pre, 0.0))
        act = jnp.where(pre > 0, pre, ex - 1.0)
        inv = lax.rsqrt(jnp.mean(act * act, axis=-1, keepdims=True) + NORM_EPS)
        out_ref[rs, :] = (act * inv).astype(BF16)
        cot = cot_ref[rs, :].astype(F32)
        dot = jnp.mean(act * cot, axis=-1, keepdims=True)
        gpre = inv * (cot - act * (inv * inv * dot)) * jnp.where(pre > 0, 1.0, ex)
        bsum = bsum + jnp.sum(gpre, axis=0, keepdims=True)
        gl = gpre.astype(BF16)
        gl_ref[rs, :] = gl
        base_ref[rs, :] = lax.dot_general(gl, ws_ref[...], nt, preferred_element_type=F32)
        eg_ref[rs, :] = (lax.dot_general(gl, wn_ref[...], nt, preferred_element_type=F32)
                         / divisor).astype(BF16)
    bg_ref[...] = bsum
    eg = eg_ref[...]
    step = min(512, ng)
    for o in range(0, rows, step):
        base_ref[o:o + step, :] += lax.dot_general(a_ref[:, o:o + step], eg, tn,
                                                   preferred_element_type=F32)
    for o in range(0, nh, step):
        hubg_ref[o:o + step, :] = lax.dot_general(a_ref[:, rows + o:rows + o + step], eg, tn,
                                                  preferred_element_type=F32).astype(BF16)
    for o in range(0, ng, step):
        halog_ref[o:o + step, :] = lax.dot_general(a_ref[:, rows + nh + o:rows + nh + o + step], eg, tn,
                                                   preferred_element_type=F32).astype(BF16)
    gl = gl_ref[...]
    wg_ref[:width, :] = lax.dot_general(feats_ref[...], gl, tn, preferred_element_type=F32).astype(BF16)
    wg_ref[width:, :] = lax.dot_general(nm_ref[...], gl, tn, preferred_element_type=F32).astype(BF16)


def bwd_exchange_kernel(g_ref, hubg_ref, wg_ref, bg_ref, r_ref, own_ref, wfull_ref,
                        t_ref, hubc, wc, bc, hub1, w1, b1, hubp, wp, bp, zsend, zrecv, wz, wrow,
                        own_sem, z_ss, z_rs, x_ss, x_rs, c_ss, c_rs, p_ss, p_rs, q_ss, q_rs,
                        az_ss, az_rs, ap_ss, ap_rs, ac_ss, ac_rs):
    x, z, c, y = coords()
    xc = x * NC + c
    yx = y * NX + x
    barrier, nbar = entry_barrier_signal(x, z, c, y)
    sib = dev(x, z, 1 - c, y)
    own = pltpu.make_async_copy(g_ref.at[z], t_ref.at[z], own_sem.at[0])
    own.start()
    pl.semaphore_wait(barrier, nbar)

    cs = [rcopy(hubg_ref.at[1 - c], hubc, c_ss.at[0], c_rs.at[0], sib),
          rcopy(wg_ref.at[1 - c], wc, c_ss.at[1], c_rs.at[1], sib),
          rcopy(bg_ref, bc, c_ss.at[2], c_rs.at[2], sib)]
    for cp in cs:
        cp.start()
    st1 = [rcopy(g_ref.at[(z + i) % NZ], t_ref.at[z], z_ss.at[i - 1], z_rs.at[i - 1], p)
           for i, p in enumerate(z_peers(x, z, c, y), 1)]
    for cp in st1:
        cp.start()
    for cp in cs:
        cp.wait_recv()
    hub1[...] = (hubg_ref[c].astype(F32) + hubc[...].astype(F32)).astype(BF16)
    w1[...] = (wg_ref[c].astype(F32) + wc[...].astype(F32)).astype(BF16)
    b1[...] = bg_ref[...] + bc[...]
    ps = []
    for i, p in enumerate(yx_peers(x, z, c, y), 1):
        pyx = ((y + i // NX) % NY) * NX + (x + i % NX) % NX
        ps.append(rcopy(hub1.at[pyx], hubp.at[i - 1], p_ss.at[0, i - 1], p_rs.at[0, i - 1], p))
        ps.append(rcopy(w1.at[pyx], wp.at[i - 1], p_ss.at[1, i - 1], p_rs.at[1, i - 1], p))
        ps.append(rcopy(b1, bp.at[i - 1], p_ss.at[2, i - 1], p_rs.at[2, i - 1], p))
    for cp in ps:
        cp.start()
    for cp in ps:
        cp.wait_recv()
    hub = hub1[yx].astype(F32)
    w = w1[yx].astype(F32)
    bias = b1[...]
    for i in range(NYX - 1):
        hub = hub + hubp[i].astype(F32)
        w = w + wp[i].astype(F32)
        bias = bias + bp[i]
    for i in range(NZ):
        zsend[i, 0:2, :] = hub[2 * i:2 * i + 2, :]
        zsend[i, 2:3, :] = w[i:i + 1, :]
        zsend[i, 3:4, :] = bias
    qs = [rcopy(zsend.at[(z + i) % NZ], zrecv.at[i - 1], q_ss.at[i - 1], q_rs.at[i - 1], p)
          for i, p in enumerate(z_peers(x, z, c, y), 1)]
    for cp in qs:
        cp.start()
    for cp in qs:
        cp.wait_recv()
    total = zsend[z]
    for i in range(NZ - 1):
        total = total + zrecv[i]
    own_ref[...] = total
    wrow[...] = total[2:3, :]
    az = [rcopy(wrow, wz.at[z], az_ss.at[i], az_rs.at[i], p)
          for i, p in enumerate(z_peers(x, z, c, y))]
    for cp in az:
        cp.start()
    wz[z] = total[2:3, :]
    own.wait()
    for cp in st1:
        cp.wait_recv()
    own2 = pltpu.make_async_copy(t_ref.at[:, xc], r_ref.at[xc], own_sem.at[1])
    own2.start()
    st2 = []
    for i, p in enumerate(xc_peers(x, z, c, y), 1):
        pxc = ((x + i // NC) % NX) * NC + (c + i % NC) % NC
        st2.append(rcopy(t_ref.at[:, pxc], r_ref.at[xc], x_ss.at[i - 1], x_rs.at[i - 1], p))
    for cp in st2:
        cp.start()
    for cp in az:
        cp.wait_recv()
    for i in range(NZ):
        wfull_ref[c, yx, i:i + 1, :] = wz[i]
    ap = [rcopy(wfull_ref.at[c, yx], wfull_ref.at[c, yx], ap_ss.at[i], ap_rs.at[i], p)
          for i, p in enumerate(yx_peers(x, z, c, y))]
    for cp in ap:
        cp.start()
    for cp in ap:
        cp.wait_recv()
    ac = rcopy(wfull_ref.at[c], wfull_ref.at[c], ac_ss, ac_rs, sib)
    ac.start()
    ac.wait_recv()
    own2.wait()
    for cp in st2:
        cp.wait_recv()
    for cp in cs + st1 + ps + qs + az + st2 + ap + [ac]:
        cp.wait_send()


def final_kernel(base_ref, ret_ref, send_ref, own_ref, hubrow_ref, wfull_ref,
                 grad_ref, us_ref, un_ref, ub_ref):
    rows, width = base_ref.shape
    lists = send_ref.shape[1]
    node = lax.broadcasted_iota(jnp.int32, (rows, lists), 0)
    hot = jnp.where(send_ref[...] == node, 1.0, 0.0).astype(BF16)
    total = base_ref[...] + jnp.dot(hot, ret_ref[...], preferred_element_type=F32)
    row = lax.broadcasted_iota(jnp.int32, (rows, 1), 0)
    for i in range(2):
        total = total + jnp.where(row == hubrow_ref[i], own_ref[i:i + 1, :], 0.0)
    grad_ref[...] = total.astype(BF16)
    for o, ref in ((0, us_ref), (width, un_ref)):
        w = wfull_ref[o:o + width, :]
        ref[...] = w * lax.rsqrt(jnp.mean(w * w) + UNIT_EPS)
    bias = own_ref[3:4, :]
    ub_ref[...] = bias * lax.rsqrt(jnp.mean(bias * bias) + UNIT_EPS)


def vmem():
    return pl.BlockSpec(memory_space=pltpu.VMEM)


def sds(shape, dtype):
    return jax.ShapeDtypeStruct(shape, dtype)


LIMIT = 48 << 20


def on_device(feats, w_self, w_neigh, bias, out_cot, degree, edge_src, hub_rows, send_rows):
    rows, width = feats.shape
    hubs = 2 * NC * NYX * NZ
    halos = 4 * NXC * NZ
    slots = rows + hubs + halos
    dma = pltpu.SemaphoreType.DMA
    send_order = send_rows.reshape(NX, NZ, NC, 4).transpose(0, 2, 1, 3).reshape(halos)
    hub_col = jnp.concatenate([hub_rows, jnp.full((6,), -1, jnp.int32)]).reshape(8, 1)
    deg_col = degree.reshape(rows, 1)

    outgoing, hub_own = pl.pallas_call(
        pick_kernel,
        out_shape=(sds((halos, width), BF16), sds((2, width), F32)),
        in_specs=[vmem()] * 3, out_specs=(vmem(),) * 2,
        compiler_params=pltpu.CompilerParams(vmem_limit_bytes=LIMIT),
    )(feats, send_order.reshape(halos, 1), hub_col)

    halo, hubtab, a = pl.pallas_call(
        fwd_exchange_kernel,
        out_shape=(sds((NZ, NXC, 4, width), BF16), sds((NC, NYX, 2 * NZ, width), BF16),
                   sds((rows, slots), BF16)),
        in_specs=[vmem()] * 4, out_specs=(vmem(),) * 3,
        scratch_shapes=[
            pltpu.VMEM((NZ, NXC, 4, width), BF16), pltpu.VMEM((NZ, 2, width), F32),
            pltpu.VMEM((2 * NZ, width), F32), pltpu.VMEM(edge_src.shape, jnp.int32),
            dma((3,)), dma((NXC - 1,)), dma((NXC - 1,)), dma((NZ - 1,)), dma((NZ - 1,)),
            dma((NZ - 1,)), dma((NZ - 1,)), dma((NYX - 1,)), dma((NYX - 1,)), dma, dma],
        compiler_params=pltpu.CompilerParams(
            collective_id=0, has_side_effects=True, vmem_limit_bytes=LIMIT),
    )(outgoing.reshape(NXC, NZ, 4, width), hub_own, edge_src, deg_col)

    outputs, base, hubg, halog, wg, bg = pl.pallas_call(
        layer_kernel,
        out_shape=(sds((rows, width), BF16), sds((rows, width), F32), sds((hubs, width), BF16),
                   sds((halos, width), BF16), sds((2 * width, width), BF16), sds((1, width), F32)),
        in_specs=[vmem()] * 9, out_specs=(vmem(),) * 6,
        scratch_shapes=[pltpu.VMEM((rows, width), BF16)] * 3,
        compiler_params=pltpu.CompilerParams(vmem_limit_bytes=LIMIT),
    )(feats, hubtab.reshape(hubs, width), halo.reshape(halos, width), a, w_self, w_neigh,
      bias.reshape(1, width), out_cot, deg_col)

    wrows = 2 * width // (NC * NYX)
    assert wrows == NZ
    back, own, wfull = pl.pallas_call(
        bwd_exchange_kernel,
        out_shape=(sds((NXC, NZ, 4, width), BF16), sds((4, width), F32),
                   sds((NC, NYX, wrows, width), F32)),
        in_specs=[vmem()] * 4, out_specs=(vmem(),) * 3,
        scratch_shapes=[
            pltpu.VMEM((NZ, NXC, 4, width), BF16),
            pltpu.VMEM((NYX, 2 * NZ, width), BF16), pltpu.VMEM((NYX, wrows, width), BF16),
            pltpu.VMEM((1, width), F32),
            pltpu.VMEM((NYX, 2 * NZ, width), BF16), pltpu.VMEM((NYX, wrows, width), BF16),
            pltpu.VMEM((1, width), F32),
            pltpu.VMEM((NYX - 1, 2 * NZ, width), BF16), pltpu.VMEM((NYX - 1, wrows, width), BF16),
            pltpu.VMEM((NYX - 1, 1, width), F32),
            pltpu.VMEM((NZ, 4, width), F32), pltpu.VMEM((NZ - 1, 4, width), F32),
            pltpu.VMEM((NZ, 1, width), F32), pltpu.VMEM((1, width), F32),
            dma((2,)), dma((NZ - 1,)), dma((NZ - 1,)), dma((NXC - 1,)), dma((NXC - 1,)),
            dma((3,)), dma((3,)), dma((3, NYX - 1)), dma((3, NYX - 1)),
            dma((NZ - 1,)), dma((NZ - 1,)), dma((NZ - 1,)), dma((NZ - 1,)),
            dma((NYX - 1,)), dma((NYX - 1,)), dma, dma],
        compiler_params=pltpu.CompilerParams(
            collective_id=1, has_side_effects=True, vmem_limit_bytes=LIMIT),
    )(halog.reshape(NZ, NXC, 4, width), hubg.reshape(NC, NYX, 2 * NZ, width),
      wg.reshape(NC, NYX, wrows, width), bg)

    smem = pl.BlockSpec(memory_space=pltpu.SMEM)
    grad, us, un, ub = pl.pallas_call(
        final_kernel,
        out_shape=(sds((rows, width), BF16), sds((width, width), F32), sds((width, width), F32),
                   sds((1, width), F32)),
        in_specs=[vmem()] * 4 + [smem] + [vmem()], out_specs=(vmem(),) * 4,
        compiler_params=pltpu.CompilerParams(vmem_limit_bytes=LIMIT),
    )(base, back.reshape(halos, width), send_order.reshape(1, halos), own, hub_rows,
      wfull.reshape(2 * width, width))
    return outputs, grad, us, un, ub.reshape(width)


def solution(mesh):
    both = ("dom", "rep")
    placed = (P(both, None), P(), P(), P(), P(both, None), P(both), P(both, None), P(both),
              P(both, None))
    return jax.shard_map(
        on_device,
        mesh=mesh,
        in_specs=placed,
        out_specs=(P(both, None), P(both, None), P(), P(), P()),
        check_vma=False,
    )
```

time: 902 us -> 108 us (0.12)
  waiting for transfers between devices: 346 us -> 0 us
  blocking collectives: 303 us -> 0 us
  other arithmetic: 106 us -> 0 us
  Pallas kernels: 0 us -> 95.3 us
  local copies, waits for them, and re-layouts: 85.4 us -> 11.9 us
  starting transfers between devices: 37 us -> 0 us
  between operations: 16.5 us -> 0.76 us
    unnamed x2 -> x0, waiting for transfers between devices: 346 us -> none
    all_gather x1 -> x0, blocking collectives: 198 us -> none  [on_device(): hub_table = lax.all_gather(hub_own, ('dom', 'rep'), axis=0, tiled=True)]
    psum x1 -> x0, blocking collectives: 105 us -> none  [on_device(): lax.psum((wself_part, wneigh_part, bias_part), ('dom', 'rep'))]
    pallas_call x0 -> x5, Pallas kernels: none -> 95.3 us  [the longest x1 42.3 us: on_device(): pl.pallas_call(fwd_exchange_kernel, out_shape=(sds((NZ, NXC, 4, width), B...]
    scatter-add x3 -> x0, other arithmetic: 67.1 us -> none  [the longest x1 62.1 us: on_device(): slot_grad = jnp.zeros((slot_table.shape[0], feat_width), jnp.float32).at[...]
    gather x5 -> x0, local copies, waits for them, and re-layouts: 54.9 us -> none  [the longest x2 51.5 us: on_device(): gathered = jnp.where(live_mask[:, :, None], slot_table[edge_src], zero_half)]
    all_to_all x2 -> x0, starting transfers between devices: 37 us -> none  [the longest x1 20.4 us: on_device(): lax.all_to_all(outgoing, 'dom', split_axis=0, concat_axis=0, tiled=True)]
    reduce_sum x5 -> x0, other arithmetic: 30.3 us -> none  [the longest x1 23.5 us: on_device(): summed = jnp.sum(gathered, axis=1, dtype=jnp.float32)]
  transfers between devices with their start and end apart: 3 -> 0, of which waited for: 1 -> 0; matrix products, arithmetic and copies ran while one was open for 2% -> 0% of each run, Pallas kernels for 0% -> 0%
where the time goes in v1:
time: 108 us
  Pallas kernels  95.3 us (88%)
  local copies, waits for them, and re-layouts  11.9 us (11%)
    pallas_call x1, Pallas kernels, on_device(): pl.pallas_call(fwd_exchange_kernel, out_shape=(sds((NZ, NXC, 4, width), B...  42.3 us
    pallas_call x1, Pallas kernels, on_device(): pl.pallas_call(bwd_exchange_kernel, out_shape=(sds((NXC, NZ, 4, width), B...  40.9 us
    pallas_call x1, Pallas kernels, on_device(): pl.pallas_call(layer_kernel, out_shape=(sds((rows, width), BF16), sds((ro...  9.26 us
    unnamed x22, local copies, waits for them, and re-layouts  8.76 us

profile of v1, /device:TPU:1, one launch (start us, length us, event | category | flops | bytes accessed | tf_op | source)
XLA Modules:
  0.0 108.0 jit_solution(10643079393979796578)
XLA Ops:
  0.6 0.7 pad_bitcast_fusion
  1.4 0.1 copy.20.hub_ref
  1.4 0.8 copy.17
  2.2 0.1 reshape_reshape.7.send_ref
  2.3 0.1 reshape_reshape.8.send_ref
  2.5 1.0 copy-done
  3.5 0.6 shard_map.128
  4.2 0.1 reshape.51.s_ref
  4.2 0.9 copy.22.deg_ref
  5.2 1.1 copy.21.edge_ref
  6.2 42.3 %shard_map.129 = (bf16[16,8,4,256]{3,2,1,0:T(4,128)(2,1)S(1)}, bf16[2,16,32,256]{3,2,1,0:T(8,128)(2,1)S(1)}, bf16[1024,2560]{1,0:T(8,128)(2,1)}) custom-call(bf16[8,16,4,256]{3,2,1,0:T(4,128)(2,1)S(1)} %reshape.51.s_ref, f32[2,256]{1,0:T(2,128)S(1)} %get-tuple-element.24.hub_ref, s32[1024,10]{1,0:T(8,128)S(1)} %copy.21.edge_ref, s32[1024,1]{1,0:T(8,128)S(1)} %copy.22.deg_ref), custom_call_target="tpu_custom_call" | custom-call | tf_op jit(solution)/shard_map/pallas_call | solution.py:351
  48.6 0.1 reshape.54.halo_ref
  48.7 1.0 copy-done.2
  49.7 0.9 copy-done.6
  50.6 0.9 copy-done.7
  51.5 0.7 copy-done.8
  52.2 9.3 %shard_map.130 = (bf16[1024,256]{1,0:T(8,128)(2,1)}, f32[1024,256]{1,0:T(8,128)S(1)}, bf16[1024,256]{1,0:T(8,128)(2,1)S(1)}, bf16[512,256]{1,0:T(8,128)(2,1)S(1)...) custom-call(bf16[1024,256]{1,0:T(8,128)(2,1)S(1)} %copy-done.1, bf16[1024,256]{1,0:T(8,128)(2,1)S(1)} %bitcast.16, ...), custom_call_target="tpu_custom_call" | custom-call | tf_op jit(solution)/shard_map/pallas_call | solution.py:365
  61.4 0.7 copy-done.3
  62.1 0.7 copy-done.5
  62.8 1.0 reshape.56.g_ref
  63.9 0.9 copy-done.4
  64.8 40.9 %shard_map.131 = (bf16[8,16,4,256]{3,2,1,0:T(4,128)(2,1)S(1)}, f32[4,256]{1,0:T(4,128)S(1)}, f32[2,16,16,256]{3,2,1,0:T(8,128)S(1)}) custom-call(bf16[16,8,4,256]{3,2,1,0:T(4,128)(2,1)S(1)} %reshape.56.g_ref, bf16[2,16,32,256]{3,2,1,0:T(8,128)(2,1)S(1)} %bitcast.18, bf16[2,16,16,256]{3,2,1,0:T(8,128)(2,1)S(1)} %bitcast.19, f32[1,256]{1,0:T(1,128)S(1)} %get-tuple-element.33.bg_ref), custom_call_target="tpu_custom_call" | custom-call | tf_op jit(solution)/shard_map/pallas_call | solution.py:377
  105.8 0.1 reshape.59.ret_ref
  105.8 2.1 %shard_map.132 = (bf16[1024,256]{1,0:T(8,128)(2,1)}, f32[256,256]{1,0:T(8,128)}, f32[256,256]{1,0:T(8,128)}, f32[1,256]{1,0:T(1,128)}) custom-call(f32[1024,256]{1,0:T(8,128)S(1)} %get-tuple-element.29.base_ref, bf16[512,256]{1,0:T(8,128)(2,1)S(1)} %reshape.59.ret_ref, s32[1,512]{1,0:T(1,128)S(1)} %reshape_reshape.7.send_ref, ...), custom_call_target="tpu_custom_call" | custom-call | tf_op jit(solution)/shard_map/pallas_call | solution.py:402
  (13 shorter events, 0.0 us)
Async XLA Ops:
  0.6 48.0 %copy-start.1 = (bf16[1024,256]{1,0:T(8,128)(2,1)S(1)}, bf16[1024,256]{1,0:T(8,128)(2,1)}, u32[]{:S(2)}) copy-start(bf16[1024,256]{1,0:T(8,128)(2,1)} %feats_ref.3) | copy-start | bytes 1572868
  2.5 1.0 copy-start
  48.6 57.3 %copy-start.9 = (s32[2]{0:T(128)S(1)}, s32[2]{0:T(128)}, u32[]{:S(2)}) copy-start(s32[2]{0:T(128)} %hubrow_ref.1) | copy-start | bytes 28
  48.6 1.0 copy-start.2
  49.7 0.9 copy-start.6
  50.6 0.9 copy-start.7
  51.5 0.7 copy-start.8
  61.4 0.7 copy-start.3
  62.1 0.7 copy-start.5
  63.9 1.0 copy-start.4

commit v2 on v0

v2 whole, which is shorter than its diff:
```python
import jax
import jax.numpy as jnp
from jax import lax
from jax.experimental import pallas as pl
from jax.experimental.pallas import tpu as pltpu
from jax.sharding import PartitionSpec as P

NORM_EPS = 1e-05
UNIT_EPS = 1e-06
NX, NZ, NC, NY = 4, 16, 2, 4
NYX = NY * NX
NXC = NX * NC
MESH = pl.DeviceIdType.MESH
F32 = jnp.float32
BF16 = jnp.bfloat16


def coords():
    d = lax.axis_index("dom")
    y = lax.axis_index("rep")
    return d // (NZ * NC), (d // NC) % NZ, d % NC, y


def dev(x, z, c, y):
    return ((x * NZ + z) * NC + c, y)


def z_offsets():
    return [NZ // 2 - (j + 1) // 2 if j % 2 else NZ // 2 + j // 2 for j in range(NZ)]


def z_slot(i):
    return jnp.where(i >= NZ // 2, 2 * (i - NZ // 2), NZ - 1 - 2 * i)


def z_peers(x, z, c, y):
    return [dev(x, (z + i) % NZ, c, y) for i in range(1, NZ)]


def yx_peers(x, z, c, y):
    return [dev((x + i % NX) % NX, z, c, (y + i // NX) % NY) for i in range(1, NYX)]


def xc_peers(x, z, c, y):
    return [dev((x + i // NC) % NX, z, (c + i % NC) % NC, y) for i in range(1, NXC)]


def entry_barrier_signal(x, z, c, y):
    peers = z_peers(x, z, c, y) + xc_peers(x, z, c, y)
    peers += [p for i, p in enumerate(yx_peers(x, z, c, y), 1) if i // NX != 0]
    barrier = pltpu.get_barrier_semaphore()
    for p in peers:
        pl.semaphore_signal(barrier, inc=1, device_id=p, device_id_type=MESH)
    return barrier, len(peers)


def rcopy(src, dst, ssem, rsem, peer):
    return pltpu.make_async_remote_copy(
        src_ref=src, dst_ref=dst, send_sem=ssem, recv_sem=rsem, device_id=peer, device_id_type=MESH
    )


TN = (((0,), (0,)), ((), ()))
NT = (((1,), (1,)), ((), ()))


def hot_nodes(send_ref, rows):
    lists = send_ref.shape[1]
    node = lax.broadcasted_iota(jnp.int32, (rows, lists), 0)
    return jnp.concatenate(
        [jnp.where(send_ref[k:k + 1, :] == node, 1.0, 0.0).astype(BF16)
         for k in range(send_ref.shape[0])], axis=1)


def layer_kernel(feats_hbm, ws_hbm, wn_hbm, cot_hbm, bias_ref, deg_ref, edge_ref, send_ref, hub_ref,
                 out_ref, base_ref, ret_ref, hubown_ref, btot_ref, wfull_ref,
                 fv, wsv, wnv, cotv, eslot, at, s_ref, hown, t_ref, zbuf, z32, hubtab, h_ref,
                 acc, pre0, dvs, nmv, glv, egv,
                 g_ref, t2, hubg, wg, bg, hubc, wc, bc, hub1, w1, b1, hubp, wp, bp,
                 wz_s, wz_r, bz_s, bz_r, hz_s, hz_r,
                 in_sem, own_sem, x_ss, x_rs, z_ss, z_rs, hz_ss, hz_rs, hp_ss, hp_rs, hc_ss, hc_rs,
                 gz_ss, gz_rs, gx_ss, gx_rs, c_ss, c_rs, p_ss, p_rs, q_ss, q_rs,
                 ap_ss, ap_rs, ac_ss, ac_rs):
    x, z, c, y = coords()
    xc = x * NC + c
    yx = y * NX + x
    sib = dev(x, z, 1 - c, y)
    offs = z_offsets()
    zp = [((z + i) % NZ, dev(x, (z + i) % NZ, c, y)) for i in offs[:-1]]
    xcp = [(((x + i // NC) % NX) * NC + (c + i % NC) % NC, p)
           for i, p in enumerate(xc_peers(x, z, c, y), 1)]
    yxp = [(((y + i // NX) % NY) * NX + (x + i % NX) % NX, p)
           for i, p in enumerate(yx_peers(x, z, c, y), 1)]
    barrier, nbar = entry_barrier_signal(x, z, c, y)
    started = []

    def go(cps):
        for cp in cps:
            cp.start()
        started.extend(cps)
        return cps

    def arrive(cps):
        for cp in cps:
            cp.wait_recv()

    rows, width = fv.shape
    fan = edge_ref.shape[0]
    slots = at.shape[0]
    hubs = 2 * NC * NYX * NZ
    halos = 4 * NXC * NZ
    loads = [pltpu.make_async_copy(src, dst, in_sem.at[i]) for i, (src, dst) in enumerate(
        ((feats_hbm, fv), (ws_hbm, wsv), (wn_hbm, wnv), (cot_hbm, cotv)))]
    for cp in loads:
        cp.start()

    hot = hot_nodes(send_ref, rows)
    nhz = NZ // 2
    p = lax.broadcasted_iota(jnp.int32, (halos, halos), 0)
    q = lax.broadcasted_iota(jnp.int32, (halos, halos), 1)
    pxc = (p // (4 * nhz)) % NXC
    want = ((p % 4) * (NXC * NZ)
            + ((pxc // NC) * NZ + 2 * ((p // 4) % nhz) + p // (4 * nhz * NXC)) * NC + pxc % NC)
    perm = jnp.where(q == want, 1.0, 0.0).astype(BF16)
    loads[0].wait()
    picked = lax.dot_general(hot, fv[...], TN, preferred_element_type=F32).astype(BF16)
    picked = jnp.dot(perm, picked, preferred_element_type=F32)
    s_ref[...] = picked.reshape(2, NXC, nhz, 4, width).astype(BF16)
    sub = lax.broadcasted_iota(jnp.int32, (8, rows), 0)
    hrow = jnp.where(sub == 0, hub_ref[0], jnp.where(sub == 1, hub_ref[1], -1))
    hhot = jnp.where(hrow == lax.broadcasted_iota(jnp.int32, (8, rows), 1), 1.0, 0.0).astype(BF16)
    hown[...] = jnp.dot(hhot, fv[...], preferred_element_type=F32)[:2]

    e = edge_ref[...]
    h = e - rows
    hub_pos = ((((h // (2 * NY)) % NC * NY + (h // 2) % NY) * NX + h // (2 * NY * NC * NZ)) * NZ
               + (h // (2 * NY * NC)) % NZ) * 2 + h % 2
    g = h - hubs
    halo_pos = (((g // (4 * NC)) % NZ * NX + g // (4 * NC * NZ)) * NC + (g // 4) % NC) * 4 + g % 4
    pos = jnp.where(e < rows, e, jnp.where(e < rows + hubs, rows + hub_pos, rows + hubs + halo_pos))
    count = jnp.minimum(deg_ref[...], fan)
    live = lax.broadcasted_iota(jnp.int32, e.shape, 0) < count
    eslot[...] = jnp.where(live, pos, -1)
    dvs[...] = lax.dot_general(jnp.where(live, 1.0, 0.0).astype(BF16), jnp.ones((fan, width), BF16),
                               TN, preferred_element_type=F32)

    nb = 128 if rows % 128 == 0 else 64
    i16 = jnp.int16

    def build(lo, hi):
        def body(j, carry):
            c0 = pl.multiple_of(j * nb, nb)
            sl = lax.broadcasted_iota(jnp.int32, (16, nb), 0)
            diff = [(jnp.broadcast_to(eslot[k:k + 1, pl.ds(c0, nb)], (16, nb)) - sl).astype(i16)
                    for k in range(fan)]
            for t in range(slots // 16):
                tot = None
                for k in range(fan):
                    one = jnp.where(diff[k] == i16(t * 16), BF16(1.0), BF16(0.0))
                    tot = one if tot is None else tot + one
                at[t * 16:(t + 1) * 16, pl.ds(c0, nb)] = tot
            return carry
        lax.fori_loop(lo, hi, body, 0)

    nblk = rows // nb
    cuts = [0, nblk * 3 // 8, nblk * 5 // 8, nblk]

    zb = pltpu.make_async_copy(hown, zbuf.at[z], own_sem.at[0])
    zb.start()
    parts = [(z + m) % 2 for m in (0, 1)]
    own1 = [pltpu.make_async_copy(s_ref.at[par, xc], t_ref.at[par, :, xc], own_sem.at[1 + m])
            for m, par in enumerate(parts)]
    for cp in own1:
        cp.start()
    build(cuts[0], cuts[1])
    pl.semaphore_wait(barrier, nbar)
    st1 = [go([rcopy(s_ref.at[par, k], t_ref.at[par, :, xc], x_ss.at[m, i], x_rs.at[m, i], d)
               for i, (k, d) in enumerate(xcp)]) for m, par in enumerate(parts)]
    hz = go([rcopy(hown, zbuf.at[z], hz_ss.at[i], hz_rs.at[i], d) for i, (k, d) in enumerate(zp)])
    build(cuts[1], cuts[2])
    st2 = []
    own2 = pltpu.make_async_copy(t_ref.at[z % 2, z // 2], h_ref.at[z], own_sem.at[3])
    for m in (0, 1):
        own1[m].wait()
        arrive(st1[m])
        st2 += go([rcopy(t_ref.at[k % 2, k // 2], h_ref.at[z], z_ss.at[j], z_rs.at[j], d)
                   for j, (k, d) in enumerate(zp) if offs[j] % 2 == m])
        if m == 0:
            own2.start()
    zb.wait()
    arrive(hz)
    for i in range(NZ):
        z32[2 * i:2 * i + 2, :] = zbuf[i]
    hubtab[c, yx] = z32[...].astype(BF16)
    hp = go([rcopy(hubtab.at[c, yx], hubtab.at[c, yx], hp_ss.at[i], hp_rs.at[i], d)
             for i, (k, d) in enumerate(yxp)])
    build(cuts[2], cuts[3])
    arrive(hp)
    hc = go([rcopy(hubtab.at[c], hubtab.at[c], hc_ss, hc_rs, sib)])
    for cp in loads[1:]:
        cp.wait()
    blk = min(256, rows)
    spans = [slice(b * blk, (b + 1) * blk) for b in range(rows // blk)]
    for rs in spans:
        acc[rs, :] = lax.dot_general(at[:rows, rs], fv[...], TN, preferred_element_type=F32)
        pre0[rs, :] = jnp.dot(fv[rs, :], wsv[...], preferred_element_type=F32) + bias_ref[...]
    arrive(hc)
    hub_rows = hubtab[...].reshape(hubs, width)
    for rs in spans:
        acc[rs, :] += lax.dot_general(at[rows:rows + hubs, rs], hub_rows, TN,
                                      preferred_element_type=F32)
    own2.wait()
    arrive(st2)

    halo = h_ref[...].reshape(halos, width)
    bsum = jnp.zeros((1, width), F32)
    for rs in spans:
        summed = acc[rs, :] + lax.dot_general(at[rows + hubs:, rs], halo, TN,
                                              preferred_element_type=F32)
        nm = (summed / dvs[rs, :]).astype(BF16)
        nmv[rs, :] = nm
        pre = pre0[rs, :] + jnp.dot(nm, wnv[...], preferred_element_type=F32)
        ex = jnp.exp(jnp.minimum(pre, 0.0))
        act = jnp.where(pre > 0, pre, ex - 1.0)
        inv = lax.rsqrt(jnp.mean(act * act, axis=-1, keepdims=True) + NORM_EPS)
        out_ref[rs, :] = (act * inv).astype(BF16)
        cot = cotv[rs, :].astype(F32)
        dot = jnp.mean(act * cot, axis=-1, keepdims=True)
        gpre = inv * (cot - act * (inv * inv * dot)) * jnp.where(pre > 0, 1.0, ex)
        bsum = bsum + jnp.sum(gpre, axis=0, keepdims=True)
        glv[rs, :] = gpre.astype(BF16)
    bg[...] = bsum
    gl = glv[...]
    wrows = wg.shape[1] * wg.shape[2]
    wpart = jnp.concatenate(
        [lax.dot_general(fv[...], gl, TN, preferred_element_type=F32),
         lax.dot_general(nmv[...], gl, TN, preferred_element_type=F32)], axis=0)
    wg[...] = wpart.reshape(wg.shape).astype(BF16)
    cw = go([rcopy(wg.at[1 - c], wc, c_ss.at[0], c_rs.at[0], sib),
             rcopy(bg, bc, c_ss.at[1], c_rs.at[1], sib)])
    for rs in spans:
        egv[rs, :] = (lax.dot_general(glv[rs, :], wnv[...], NT, preferred_element_type=F32)
                      / dvs[rs, :]).astype(BF16)
    eg = egv[...]

    halo_grad = jnp.dot(at[rows + hubs:, :], eg, preferred_element_type=F32)
    g_ref[...] = halo_grad.reshape(NZ, NXC, 4, width).astype(BF16)
    own3 = pltpu.make_async_copy(g_ref.at[z], t2.at[NZ - 1], own_sem.at[4])
    own3.start()
    gz = go([rcopy(g_ref.at[k], t2.at[j], gz_ss.at[j], gz_rs.at[j], d)
             for j, (k, d) in enumerate(zp)])
    arrive(cw)
    w1[...] = (wg[c].astype(F32) + wc[...].astype(F32)).astype(BF16)
    b1[...] = bg[...] + bc[...]
    pw = []
    for i, (k, d) in enumerate(yxp):
        pw += go([rcopy(w1.at[k], wp.at[i], p_ss.at[0, i], p_rs.at[0, i], d),
                  rcopy(b1, bp.at[i], p_ss.at[1, i], p_rs.at[1, i], d)])
    hub_grad = jnp.dot(at[rows:rows + hubs, :], eg, preferred_element_type=F32)
    hubg[...] = hub_grad.reshape(hubg.shape).astype(BF16)
    ch = go([rcopy(hubg.at[1 - c], hubc, c_ss.at[2], c_rs.at[2], sib)])
    arrive(ch)
    hub1[...] = (hubg[c].astype(F32) + hubc[...].astype(F32)).astype(BF16)
    ph = go([rcopy(hub1.at[k], hubp.at[i], p_ss.at[2, i], p_rs.at[2, i], d)
             for i, (k, d) in enumerate(yxp)])
    arrive(pw)
    w = w1[yx].astype(F32)
    bias = b1[...]
    for i in range(NYX - 1):
        w = w + wp[i].astype(F32)
        bias = bias + bp[i]
    wz_s[...] = w.astype(BF16)
    bz_s[...] = bias
    zw = []
    for j, (k, d) in enumerate(zp):
        zw += go([rcopy(wz_s, wz_r.at[j], q_ss.at[0, j], q_rs.at[0, j], d),
                  rcopy(bz_s, bz_r.at[j], q_ss.at[1, j], q_rs.at[1, j], d)])
    base_ref[...] = (lax.dot_general(gl, wsv[...], NT, preferred_element_type=F32)
                     + jnp.dot(at[:rows, :], eg, preferred_element_type=F32))
    arrive(ph)
    hub = hub1[yx].astype(F32)
    for i in range(NYX - 1):
        hub = hub + hubp[i].astype(F32)
    for i in range(NZ):
        hz_s[i] = hub[2 * i:2 * i + 2, :]
    zh = go([rcopy(hz_s.at[k], hz_r.at[j], q_ss.at[2, j], q_rs.at[2, j], d)
             for j, (k, d) in enumerate(zp)])
    half = NZ // 2
    gx = []
    own4 = []
    for m in (0, 1):
        arrive(gz[m * half:(m + 1) * half])
        if m:
            own3.wait()
        part = pl.ds(m * half, half)
        cp = pltpu.make_async_copy(t2.at[part, xc], ret_ref.at[xc, part], own_sem.at[5 + m])
        cp.start()
        own4.append(cp)
        gx += go([rcopy(t2.at[part, k], ret_ref.at[xc, part], gx_ss.at[m, i], gx_rs.at[m, i], d)
                  for i, (k, d) in enumerate(xcp)])
    arrive(zw)
    w = wz_s[...].astype(F32)
    bias = bz_s[...]
    for j in range(NZ - 1):
        w = w + wz_r[j].astype(F32)
        bias = bias + bz_r[j]
    btot_ref[...] = bias
    wfull_ref[c, yx] = w.astype(BF16)
    ap = go([rcopy(wfull_ref.at[c, yx], wfull_ref.at[c, yx], ap_ss.at[i], ap_rs.at[i], d)
             for i, (k, d) in enumerate(yxp)])
    arrive(zh)
    own = hz_s[z]
    for j in range(NZ - 1):
        own = own + hz_r[j]
    hubown_ref[...] = own
    arrive(ap)
    ac = go([rcopy(wfull_ref.at[c], wfull_ref.at[c], ac_ss, ac_rs, sib)])
    for cp in own4:
        cp.wait()
    arrive(gx)
    arrive(ac)
    for cp in started:
        cp.wait_send()


def final_kernel(base_ref, ret_ref, send_ref, own_ref, hubrow_ref, btot_ref, wfull_ref,
                 grad_ref, us_ref, un_ref, ub_ref):
    rows, width = base_ref.shape
    halos = 4 * NXC * NZ
    z = coords()[1]
    p = lax.broadcasted_iota(jnp.int32, (halos, halos), 0)
    q = lax.broadcasted_iota(jnp.int32, (halos, halos), 1)
    e = p % (NXC * NZ)
    back = (z - (e // NC) % NZ + NZ) % NZ
    want = ((((e // (NC * NZ)) * NC + e % NC) * NZ) + z_slot(back)) * 4 + p // (NXC * NZ)
    perm = jnp.where(q == want, 1.0, 0.0).astype(BF16)
    ret = ret_ref[...].reshape(halos, width)
    ret = jnp.dot(perm, ret, preferred_element_type=F32).astype(BF16)
    total = base_ref[...] + jnp.dot(hot_nodes(send_ref, rows), ret, preferred_element_type=F32)
    row = lax.broadcasted_iota(jnp.int32, (rows, 1), 0)
    for i in range(2):
        total = total + jnp.where(row == hubrow_ref[i], own_ref[i:i + 1, :], 0.0)
    grad_ref[...] = total.astype(BF16)
    w = wfull_ref[...].reshape(2 * width, width).astype(F32)
    for o, ref in ((0, us_ref), (width, un_ref)):
        part = w[o:o + width, :]
        ref[...] = part * lax.rsqrt(jnp.mean(part * part) + UNIT_EPS)
    bias = btot_ref[...]
    ub_ref[...] = bias * lax.rsqrt(jnp.mean(bias * bias) + UNIT_EPS)


def vmem():
    return pl.BlockSpec(memory_space=pltpu.VMEM)


def sds(shape, dtype):
    return jax.ShapeDtypeStruct(shape, dtype)


LIMIT = 56 << 20


def on_device(feats, w_self, w_neigh, bias, out_cot, degree, edge_src, hub_rows, send_rows):
    rows, width = feats.shape
    hubs = 2 * NC * NYX * NZ
    halos = 4 * NXC * NZ
    slots = rows + hubs + halos
    fan = edge_src.shape[1]
    wrows = 2 * width // (NC * NYX)
    nhz = NZ // 2
    dma = pltpu.SemaphoreType.DMA
    smem = pl.BlockSpec(memory_space=pltpu.SMEM)
    hbm = pl.BlockSpec(memory_space=pl.ANY)

    def vb(*shape):
        return pltpu.VMEM(shape, BF16)

    def vf(*shape):
        return pltpu.VMEM(shape, F32)

    send_t = send_rows.T
    outputs, base, ret, hubown, btot, wfull = pl.pallas_call(
        layer_kernel,
        out_shape=(sds((rows, width), BF16), sds((rows, width), F32), sds((NXC, NZ, 4, width), BF16),
                   sds((2, width), F32), sds((1, width), F32), sds((NC, NYX, wrows, width), BF16)),
        in_specs=[hbm] * 4 + [vmem()] * 4 + [smem], out_specs=(vmem(),) * 6,
        scratch_shapes=[
            vb(rows, width), vb(width, width), vb(width, width), vb(rows, width),
            pltpu.VMEM((fan, rows), jnp.int32), vb(slots, rows),
            vb(2, NXC, nhz, 4, width), vf(2, width), vb(2, nhz, NXC, 4, width), vf(NZ, 2, width),
            vf(2 * NZ, width), vb(NC, NYX, 2 * NZ, width), vb(NZ, NXC, 4, width),
            vf(rows, width), vf(rows, width), vf(rows, width),
            vb(rows, width), vb(rows, width), vb(rows, width),
            vb(NZ, NXC, 4, width), vb(NZ, NXC, 4, width),
            vb(NC, NYX, 2 * NZ, width), vb(NC, NYX, wrows, width), vf(1, width),
            vb(NYX, 2 * NZ, width), vb(NYX, wrows, width), vf(1, width),
            vb(NYX, 2 * NZ, width), vb(NYX, wrows, width), vf(1, width),
            vb(NYX - 1, 2 * NZ, width), vb(NYX - 1, wrows, width), vf(NYX - 1, 1, width),
            vb(wrows, width), vb(NZ - 1, wrows, width), vf(1, width), vf(NZ - 1, 1, width),
            vf(NZ, 2, width), vf(NZ - 1, 2, width),
            dma((4,)), dma((7,)), dma((2, NXC - 1)), dma((2, NXC - 1)), dma((NZ - 1,)), dma((NZ - 1,)),
            dma((NZ - 1,)), dma((NZ - 1,)), dma((NYX - 1,)), dma((NYX - 1,)), dma, dma,
            dma((NZ - 1,)), dma((NZ - 1,)), dma((2, NXC - 1)), dma((2, NXC - 1)),
            dma((3,)), dma((3,)), dma((3, NYX - 1)), dma((3, NYX - 1)),
            dma((3, NZ - 1)), dma((3, NZ - 1)),
            dma((NYX - 1,)), dma((NYX - 1,)), dma, dma],
        compiler_params=pltpu.CompilerParams(
            collective_id=0, has_side_effects=True, vmem_limit_bytes=LIMIT),
    )(feats, w_self, w_neigh, out_cot, bias.reshape(1, width), degree.reshape(1, rows), edge_src.T,
      send_t, hub_rows)

    grad, us, un, ub = pl.pallas_call(
        final_kernel,
        out_shape=(sds((rows, width), BF16), sds((width, width), F32), sds((width, width), F32),
                   sds((1, width), F32)),
        in_specs=[vmem()] * 4 + [smem] + [vmem()] * 2, out_specs=(vmem(),) * 4,
        compiler_params=pltpu.CompilerParams(vmem_limit_bytes=LIMIT),
    )(base, ret, send_t, hubown, hub_rows, btot, wfull)
    return outputs, grad, us, un, ub.reshape(width)


def solution(mesh):
    both = ("dom", "rep")
    placed = (P(both, None), P(), P(), P(), P(both, None), P(both), P(both, None), P(both),
              P(both, None))
    return jax.shard_map(
        on_device,
        mesh=mesh,
        in_specs=placed,
        out_specs=(P(both, None), P(both, None), P(), P(), P()),
        check_vma=False,
    )
```

time: 902 us -> 76.5 us (0.08)
  waiting for transfers between devices: 346 us -> 0 us
  blocking collectives: 303 us -> 0 us
  other arithmetic: 106 us -> 0 us
  local copies, waits for them, and re-layouts: 85.4 us -> 0.8 us
  Pallas kernels: 0 us -> 74.9 us
  starting transfers between devices: 37 us -> 0 us
  between operations: 16.5 us -> 0.65 us
    unnamed x2 -> x0, waiting for transfers between devices: 346 us -> none
    all_gather x1 -> x0, blocking collectives: 198 us -> none  [on_device(): hub_table = lax.all_gather(hub_own, ('dom', 'rep'), axis=0, tiled=True)]
    psum x1 -> x0, blocking collectives: 105 us -> none  [on_device(): lax.psum((wself_part, wneigh_part, bias_part), ('dom', 'rep'))]
    pallas_call x0 -> x2, Pallas kernels: none -> 74.9 us  [the longest x1 71.3 us: on_device(): pl.pallas_call(layer_kernel, out_shape=(sds((rows, width), BF16), sds((ro...]
    scatter-add x3 -> x0, other arithmetic: 67.1 us -> none  [the longest x1 62.1 us: on_device(): slot_grad = jnp.zeros((slot_table.shape[0], feat_width), jnp.float32).at[...]
    gather x5 -> x0, local copies, waits for them, and re-layouts: 54.9 us -> none  [the longest x2 51.5 us: on_device(): gathered = jnp.where(live_mask[:, :, None], slot_table[edge_src], zero_half)]
    all_to_all x2 -> x0, starting transfers between devices: 37 us -> none  [the longest x1 20.4 us: on_device(): lax.all_to_all(outgoing, 'dom', split_axis=0, concat_axis=0, tiled=True)]
    reduce_sum x5 -> x0, other arithmetic: 30.3 us -> none  [the longest x1 23.5 us: on_device(): summed = jnp.sum(gathered, axis=1, dtype=jnp.float32)]
  transfers between devices with their start and end apart: 3 -> 0, of which waited for: 1 -> 0; matrix products, arithmetic and copies ran while one was open for 2% -> 0% of each run, Pallas kernels for 0% -> 0%
where the time goes in v2:
time: 76.5 us; the launch traced here: 76.3 us
  Pallas kernels  74.9 us (98%)
  local copies, waits for them, and re-layouts  0.8 us (1%)
    pallas_call x1, Pallas kernels, on_device(): pl.pallas_call(layer_kernel, out_shape=(sds((rows, width), BF16), sds((ro...  71.3 us
    pallas_call x1, Pallas kernels, on_device(): pl.pallas_call(final_kernel, out_shape=(sds((rows, width), BF16), sds((wi...  3.53 us

profile of v2, /device:TPU:1, one launch (start us, length us, event | category | flops | bytes accessed | tf_op | source)
XLA Modules:
  0.0 76.3 jit_solution(1529527156236578079)
XLA Ops:
  0.6 71.3 %shard_map.128 = (bf16[1024,256]{1,0:T(8,128)(2,1)}, f32[1024,256]{1,0:T(8,128)}, bf16[8,16,4,256]{3,2,1,0:T(4,128)(2,1)}, f32[2,256]{1,0:T(2,128)}, f32[1,256]{1,0:T(1,128)}, /*index=5*/bf16[2,16,16,256]{3,2,1,0:T(8,128)(2,1)}) custom-call(bf16[1024,256]{1,0:T(8,128)(2,1)} %feats_hbm.1, bf16[256,256]{1,0:T(8,128)(2,1)} %ws_hbm.1, bf16[256,256]{1,0:T(8,128)(2,1)} %wn_hbm.1, ...), custom_call_target="tpu_custom_call" | custom-call | tf_op jit(solution)/shard_map/pallas_call | solution.py:382
  72.0 0.0 copy-start
  72.0 3.5 %shard_map.129 = (bf16[1024,256]{1,0:T(8,128)(2,1)}, f32[256,256]{1,0:T(8,128)}, f32[256,256]{1,0:T(8,128)}, f32[1,256]{1,0:T(1,128)}) custom-call(f32[1024,256]{1,0:T(8,128)} %get-tuple-element.16.base_ref, bf16[8,16,4,256]{3,2,1,0:T(4,128)(2,1)} %get-tuple-element.17.ret_ref, s32[4,128]{1,0:T(4,128)} %bitcast.7, f32[2,256]{1,0:T(2,128)} %get-tuple-element.18.own_ref, ...), custom_call_target="tpu_custom_call" | custom-call | tf_op jit(solution)/shard_map/pallas_call | solution.py:412
  75.5 0.0 copy-done
  75.5 0.8 %copy.15 = bf16[1024,256]{1,0:T(8,128)(2,1)} copy(bf16[1024,256]{1,0:T(8,128)(2,1)S(1)} %copy-done) | data formatting | bytes 1048576
Async XLA Ops:
  72.0 3.5 %copy-start = (bf16[1024,256]{1,0:T(8,128)(2,1)S(1)}, bf16[1024,256]{1,0:T(8,128)(2,1)}, u32[]{:S(2)}) copy-start(bf16[1024,256]{1,0:T(8,128)(2,1)} %get-tuple-element.30) | copy-start | bytes 1572868

commit v3 on v2

v3 whole, which is shorter than its diff:
```python
import jax
import jax.numpy as jnp
from jax import lax
from jax.experimental import pallas as pl
from jax.experimental.pallas import tpu as pltpu
from jax.sharding import PartitionSpec as P

NORM_EPS = 1e-05
UNIT_EPS = 1e-06
NX, NZ, NC, NY = 4, 16, 2, 4
NZL = 4
NYX = NY * NX
NXC = NX * NC
MESH = pl.DeviceIdType.MESH
F32 = jnp.float32
BF16 = jnp.bfloat16


def coords():
    d = lax.axis_index("dom")
    y = lax.axis_index("rep")
    return d // (NZ * NC), (d // NC) % NZ, d % NC, y


def dev(x, z, c, y):
    return ((x * NZ + z) * NC + c, y)


def z_offsets():
    return [NZ // 2 - (j + 1) // 2 if j % 2 else NZ // 2 + j // 2 for j in range(NZ)]


def z_peers(x, z, c, y):
    return [dev(x, (z + i) % NZ, c, y) for i in range(1, NZ)]


def yx_peers(x, z, c, y):
    return [dev((x + i % NX) % NX, z, c, (y + i // NX) % NY) for i in range(1, NYX)]


def xc_peers(x, z, c, y):
    return [dev((x + i // NC) % NX, z, (c + i % NC) % NC, y) for i in range(1, NXC)]


def entry_barrier_signal(x, z, c, y):
    peers = z_peers(x, z, c, y) + xc_peers(x, z, c, y)
    peers += [p for i, p in enumerate(yx_peers(x, z, c, y), 1) if i // NX != 0]
    barrier = pltpu.get_barrier_semaphore()
    for p in peers:
        pl.semaphore_signal(barrier, inc=1, device_id=p, device_id_type=MESH)
    return barrier, len(peers)


def rcopy(src, dst, ssem, rsem, peer):
    return pltpu.make_async_remote_copy(
        src_ref=src, dst_ref=dst, send_sem=ssem, recv_sem=rsem, device_id=peer, device_id_type=MESH
    )


TN = (((0,), (0,)), ((), ()))
NT = (((1,), (1,)), ((), ()))


def list_ids(send_ref, want):
    ids = send_ref[...]
    places, lists = ids.shape
    n = want.shape[1]
    pick = jnp.where(lax.broadcasted_iota(jnp.int32, (lists, n), 0) == want, 1.0, 0.0).astype(BF16)
    hi = jnp.dot((ids >> 5).astype(F32).astype(BF16), pick, preferred_element_type=F32)
    lo = jnp.dot((ids & 31).astype(F32).astype(BF16), pick, preferred_element_type=F32)
    place = lax.broadcasted_iota(jnp.int32, (places, n), 1) & 3
    mine = place == lax.broadcasted_iota(jnp.int32, (places, n), 0)
    return jnp.sum(jnp.where(mine, hi * 32.0 + lo, 0.0), axis=0, keepdims=True).astype(jnp.int32)


def list_ids_column(send_ref, want):
    ids = send_ref[...]
    places, lists = ids.shape
    n = want.shape[0]
    pick = jnp.where(lax.broadcasted_iota(jnp.int32, (n, lists), 1) == want, 1.0, 0.0).astype(BF16)
    both = jnp.concatenate([ids >> 5, ids & 31], axis=0).astype(F32).astype(BF16)
    got = lax.dot_general(pick, both, NT, preferred_element_type=F32)
    lane = lax.broadcasted_iota(jnp.int32, got.shape, 1)
    mine = (lax.broadcasted_iota(jnp.int32, got.shape, 0) & 3) == (lane & 3)
    got = jnp.where(lane < places, got * 32.0, got)
    return jnp.sum(jnp.where(mine, got, 0.0), axis=1, keepdims=True).astype(jnp.int32)


def div(v, n):
    return v >> (n.bit_length() - 1)


def mod(v, n):
    return v & (n - 1)


def hot_nodes(ids, rows):
    node = lax.broadcasted_iota(jnp.int32, (rows, 128 if ids.shape[1] % 128 == 0 else ids.shape[1]), 0)
    w = node.shape[1]
    return jnp.concatenate(
        [jnp.where(ids[:, o:o + w] == node, 1.0, 0.0).astype(BF16) for o in range(0, ids.shape[1], w)],
        axis=1)


class Exchange:
    def __init__(self, s0, s1, u, v, h, sems):
        self.s0, self.s1, self.u, self.v, self.h = s0, s1, u, v, h
        (self.own, self.ass, self.ars, self.bss, self.brs, self.css, self.crs, self.dss,
         self.drs) = sems
        self.x, self.z, self.c, self.y = coords()
        self.xc = self.x * NC + self.c
        x, z, c, y = self.x, self.z, self.c, self.y
        self.offs = z_offsets()
        self.zp = [((z + i) % NZ, dev(x, (z + i) % NZ, c, y)) for i in self.offs[:-1]]
        self.a = [rcopy(s0.at[k], u.at[z], self.ass.at[j], self.ars.at[j], d)
                  for j, (k, d) in enumerate(self.zp)]
        self.a_own = pltpu.make_async_copy(s0.at[z], u.at[z], self.own.at[0])
        self.cc = [rcopy(v.at[k], h.at[z], self.css.at[j], self.crs.at[j], d)
                   for j, (k, d) in enumerate(self.zp)]
        self.c_own = pltpu.make_async_copy(v.at[z], h.at[z], self.own.at[1])
        self.b = [rcopy(s1.at[(x + i) % NX], v.at[:, self.xc], self.bss.at[i],
                        self.brs.at[NC * i + c], dev((x + i) % NX, z, 1, y)) for i in range(NX)]
        self.b_own = pltpu.make_async_copy(s1.at[x], v.at[:, self.xc], self.own.at[2])
        self.d = [rcopy(u.at[:, (x + i) % NX], h.at[:, self.xc], self.dss.at[i],
                        self.drs.at[NC * i + c], dev((x + i) % NX, z, 0, y)) for i in range(NX)]
        self.d_own = pltpu.make_async_copy(u.at[:, x], h.at[:, self.xc], self.own.at[3])

    def across(self, cps, own, core, start):
        def act(cp):
            if start:
                cp.start()
            else:
                cp.wait_send()
        for cp in cps[1:]:
            act(cp)

        @pl.when(self.c != core)
        def _():
            act(cps[0])
        if start:
            @pl.when(self.c == core)
            def _():
                own.start()

    def landed(self, src, dst, ss, rs, own, core):
        for i in range(NX):
            for k in range(NC):
                if i or k != core:
                    rcopy(src, dst, ss.at[0], rs.at[NC * i + k],
                          dev((self.x + 1) % NX, self.z, 1 - self.c, self.y)).wait_recv()
        own.wait()

    def start(self):
        self.across(self.b, self.b_own, 1, True)
        for cp in self.a:
            cp.start()
        self.a_own.start()

    def turn_b(self, lo, hi):
        @pl.when(self.c == 1)
        def _():
            if lo == 0:
                self.landed(self.s1.at[0], self.v.at[:, 0], self.bss, self.brs, self.b_own, 1)
            for cp in self.cc[lo:hi]:
                cp.start()
            if hi == NZ - 1:
                self.c_own.start()

    def turn_a(self):
        for cp in self.a:
            cp.wait_recv()
        self.a_own.wait()
        self.across(self.d, self.d_own, 0, True)

    def finish(self):
        @pl.when(self.c == 1)
        def _():
            for cp in self.cc:
                cp.wait_recv()
            self.c_own.wait()

        @pl.when(self.c == 0)
        def _():
            self.landed(self.u.at[:, 0], self.h.at[:, 0], self.dss, self.drs, self.d_own, 0)

    def sent(self):
        for cp in self.a:
            cp.wait_send()
        self.across(self.b, self.b_own, 1, False)
        self.across(self.d, self.d_own, 0, False)

        @pl.when(self.c == 1)
        def _():
            for cp in self.cc:
                cp.wait_send()


def layer_kernel(feats_hbm, ws_hbm, wn_hbm, cot_hbm, bias_ref, deg_ref, edge_ref, send_ref, hub_ref,
                 out_hbm, grad_hbm, btot_ref, wfull_ref,
                 fv, wsv, wnv, cotv, eslot, at, hown, zbuf, z32, hubtab, h_ref,
                 acc, pre0, dvs, nmv, glv, egv, fvt, out_v, base_v, grad_v, ret_ref, s0, s1, u, v, g0, g1, gu, gv,
                 hubg, wg, bg, hubc, wc, bc, hub1, w1, b1, hubp, wp, bp,
                 wn_s, wn_r, wf_s, wf_r, bn_s, bn_r, bf_s, bf_r, hz_s, hz_r,
                 in_sem, hz_ss, hz_rs, hp_ss, hp_rs, hc_ss, hc_rs,
                 c_ss, c_rs, p_ss, p_rs, q_ss, q_rs, n_ss, n_rs, f_ss, f_rs,
                 ap_ss, ap_rs, ac_ss, ac_rs, *ex_sems):
    x, z, c, y = coords()
    barrier, nbar = entry_barrier_signal(x, z, c, y)
    fwd = Exchange(s0, s1, u, v, h_ref, ex_sems[:9])
    bwd = Exchange(g0, g1, gu, gv, ret_ref, ex_sems[9:])
    yx = y * NX + x
    sib = dev(x, z, 1 - c, y)
    offs = z_offsets()
    zp = [((z + i) % NZ, dev(x, (z + i) % NZ, c, y)) for i in offs[:-1]]
    yxp = [(((y + i // NX) % NY) * NX + (x + i % NX) % NX, p)
           for i, p in enumerate(yx_peers(x, z, c, y), 1)]
    started = []

    def go(cps):
        for cp in cps:
            cp.start()
        started.extend(cps)
        return cps

    def flush_part(cps):
        for cp in cps:
            cp.wait_send()
        gone = {id(cp) for cp in cps}
        started[:] = [cp for cp in started if id(cp) not in gone]

    def flush():
        for cp in started:
            cp.wait_send()
        started.clear()

    def arrive(cps):
        for cp in cps:
            cp.wait_recv()

    def pass_on(cps, buf, ss, rs):
        out = go([rcopy(buf.at[c, yx], buf.at[c, yx], ss.at[0], rs.at[0], sib)])
        for i, cp in enumerate(cps, 1):
            cp.wait_recv()
            k = ((y + NY - i // NX) % NY) * NX + (x + NX - i % NX) % NX
            out += go([rcopy(buf.at[c, k], buf.at[c, k], ss.at[i], rs.at[i], sib)])
        return out

    rows, width = fv.shape
    fan = edge_ref.shape[0]
    slots = at.shape[0]
    hubs = 2 * NC * NYX * NZ
    halos = 4 * NXC * NZ
    loads = [pltpu.make_async_copy(src, dst, in_sem.at[i]) for i, (src, dst) in enumerate(
        ((feats_hbm, fv), (ws_hbm, wsv), (wn_hbm, wnv), (cot_hbm, cotv)))]
    for cp in loads:
        cp.start()

    stores = [pltpu.make_async_copy(out_v, out_hbm, in_sem.at[5]),
              pltpu.make_async_copy(grad_v, grad_hbm, in_sem.at[6])]

    half = halos // 2
    p = lax.broadcasted_iota(jnp.int32, (halos, 1), 0)
    p2 = div(mod(p, half), 4)
    want = jnp.where(p < half, (mod(p2, NX) * NZ + div(p2, NX)) * NC, p2 * NC + 1)
    ids = list_ids_column(send_ref, want)
    hot = jnp.where(ids == lax.broadcasted_iota(jnp.int32, (halos, rows), 1), 1.0, 0.0).astype(BF16)
    loads[0].wait()
    picked = jnp.dot(hot, fv[...], preferred_element_type=F32)
    s0[...] = picked[:half].reshape(s0.shape).astype(BF16)
    s1[...] = picked[half:].reshape(s1.shape).astype(BF16)
    sub = lax.broadcasted_iota(jnp.int32, (8, rows), 0)
    hrow = jnp.where(sub == 0, hub_ref[0], jnp.where(sub == 1, hub_ref[1], -1))
    hhot = jnp.where(hrow == lax.broadcasted_iota(jnp.int32, (8, rows), 1), 1.0, 0.0).astype(BF16)
    hown[...] = jnp.dot(hhot, fv[...], preferred_element_type=F32)[:2]

    e = edge_ref[...]
    h = e - rows
    hub_pos = (((mod(div(h, 2 * NY), NC) * NY + mod(div(h, 2), NY)) * NX
                + div(h, 2 * NY * NC * NZ)) * NZ + mod(div(h, 2 * NY * NC), NZ)) * 2 + mod(h, 2)
    g = h - hubs
    halo_pos = ((mod(div(g, 4 * NC), NZ) * NX + div(g, 4 * NC * NZ)) * NC + mod(div(g, 4), NC)) * 4 + mod(g, 4)
    pos = jnp.where(e < rows, e, jnp.where(e < rows + hubs, rows + hub_pos, rows + hubs + halo_pos))
    count = jnp.minimum(deg_ref[...], fan)
    live = lax.broadcasted_iota(jnp.int32, e.shape, 0) < count
    eslot[...] = jnp.where(live, pos, -1)
    nb = 128 if rows % 128 == 0 else 64
    i16 = jnp.int16

    def build(lo, hi):
        def body(j, carry):
            c0 = pl.multiple_of(j * nb, nb)
            sl = lax.broadcasted_iota(jnp.int32, (16, nb), 0)
            diff = [(jnp.broadcast_to(eslot[k:k + 1, pl.ds(c0, nb)], (16, nb)) - sl).astype(i16)
                    for k in range(fan)]
            for t in range(slots // 16):
                tot = None
                for k in range(fan):
                    one = jnp.where(diff[k] == i16(t * 16), BF16(1.0), BF16(0.0))
                    tot = one if tot is None else tot + one
                at[t * 16:(t + 1) * 16, pl.ds(c0, nb)] = tot
            return carry
        lax.fori_loop(lo, hi, body, 0)

    nblk = rows // nb
    cuts = [0, nblk // 8, nblk * 3 // 8, nblk * 5 // 8, nblk]

    zb = pltpu.make_async_copy(hown, zbuf.at[z], in_sem.at[4])
    zb.start()
    build(cuts[0], cuts[1])
    pl.semaphore_wait(barrier, nbar)
    hz = go([rcopy(hown, zbuf.at[z], hz_ss.at[i], hz_rs.at[i], d) for i, (k, d) in enumerate(zp)])
    fwd.start()
    build(cuts[1], cuts[2])
    fvt[...] = fv[...].T
    fwd.turn_b(0, NZ - 1)
    build(cuts[2], cuts[3])
    zb.wait()
    arrive(hz)
    for i in range(NZ):
        z32[2 * i:2 * i + 2, :] = zbuf[i]
    hubtab[c, yx] = z32[...].astype(BF16)
    hp = go([rcopy(hubtab.at[c, yx], hubtab.at[c, yx], hp_ss.at[i], hp_rs.at[i], d)
             for i, (k, d) in enumerate(yxp)])
    fwd.turn_a()
    build(cuts[3], cuts[4])
    acc[...] = jnp.dot(fvt[...], at[:rows, :], preferred_element_type=F32)
    for cp in loads[1:]:
        cp.wait()
    hc = pass_on(hp, hubtab, hc_ss, hc_rs)
    blk = min(256, rows)
    spans = [slice(b * blk, (b + 1) * blk) for b in range(rows // blk)]
    for rs in spans:
        pre0[rs, :] = jnp.dot(fv[rs, :], wsv[...], preferred_element_type=F32) + bias_ref[...]
    dvs[...] = 1.0 / lax.dot_general(jnp.where(live, 1.0, 0.0).astype(BF16),
                                     jnp.ones((fan, width), BF16), TN, preferred_element_type=F32)
    rvc = 1.0 / count.astype(F32)
    arrive(hc)
    hub_rows = hubtab[...].reshape(hubs, width)
    acc[...] += jnp.dot(hub_rows.T, at[rows:rows + hubs, :], preferred_element_type=F32)
    fwd.finish()

    halo = h_ref[...].reshape(halos, width).T
    bsum = jnp.zeros((1, width), F32)
    for rs in spans:
        summed = acc[:, rs] + jnp.dot(halo, at[rows + hubs:, rs], preferred_element_type=F32)
        nmt = (summed * rvc[:, rs]).astype(BF16)
        nmv[:, rs] = nmt
        pre = pre0[rs, :] + lax.dot_general(nmt, wnv[...], TN, preferred_element_type=F32)
        ex = jnp.exp(jnp.minimum(pre, 0.0))
        act = jnp.where(pre > 0, pre, ex - 1.0)
        inv = lax.rsqrt(jnp.mean(act * act, axis=-1, keepdims=True) + NORM_EPS)
        out_v[rs, :] = (act * inv).astype(BF16)
        cot = cotv[rs, :].astype(F32)
        dot = jnp.mean(act * cot, axis=-1, keepdims=True)
        gpre = inv * (cot - act * (inv * inv * dot)) * jnp.where(pre > 0, 1.0, ex)
        bsum = bsum + jnp.sum(gpre, axis=0, keepdims=True)
        glv[rs, :] = gpre.astype(BF16)
    bg[...] = bsum
    gl = glv[...]
    wrows = wg.shape[2]
    wg[...] = jnp.concatenate(
        [jnp.dot(fvt[...], gl, preferred_element_type=F32),
         jnp.dot(nmv[...], gl, preferred_element_type=F32)], axis=0).reshape(wg.shape)
    cw = go([rcopy(wg.at[1 - c], wc, c_ss.at[0], c_rs.at[0], sib)])
    cb = go([rcopy(bg, bc, c_ss.at[1], c_rs.at[1], sib)])
    stores[0].start()
    for rs in spans:
        egv[rs, :] = (lax.dot_general(glv[rs, :], wnv[...], NT, preferred_element_type=F32)
                      * dvs[rs, :]).astype(BF16)
    eg = egv[...]
    flush_part(hz + hp + hc)

    hub_grad = jnp.dot(at[rows:rows + hubs, :], eg, preferred_element_type=F32)
    hubg[...] = hub_grad.reshape(hubg.shape).astype(BF16)
    ch = go([rcopy(hubg.at[1 - c], hubc, c_ss.at[2], c_rs.at[2], sib)])
    halo_grad = jnp.dot(at[rows + hubs:, :], eg, preferred_element_type=F32)
    halo_grad = halo_grad.reshape(NZ, NX, NC, 4, width).astype(BF16)
    g0[...] = halo_grad[:, :, 0]
    for i in range(NX):
        g1[i] = halo_grad[:, i, 1]
    arrive(cw)
    w1[...] = (wg[c] + wc[...]).astype(BF16)
    pw = go([rcopy(w1.at[k], wp.at[i], p_ss.at[0, i], p_rs.at[0, i], d)
             for i, (k, d) in enumerate(yxp)])
    bwd.start()
    arrive(ch)
    hub1[...] = (hubg[c].astype(F32) + hubc[...].astype(F32)).astype(BF16)
    ph = go([rcopy(hub1.at[k], hubp.at[i], p_ss.at[2, i], p_rs.at[2, i], d)
             for i, (k, d) in enumerate(yxp)])
    arrive(cb)
    b1[...] = bg[...] + bc[...]
    pb = go([rcopy(b1, bp.at[i], p_ss.at[1, i], p_rs.at[1, i], d) for i, (k, d) in enumerate(yxp)])
    base_v[...] = (lax.dot_general(gl, wsv[...], NT, preferred_element_type=F32)
                   + jnp.dot(at[:rows, :], eg, preferred_element_type=F32))
    arrive(pw)
    w = w1[yx].astype(F32)
    for i in range(NYX - 1):
        w = w + wp[i].astype(F32)
    wn_s[...] = w
    zlo = z % NZL
    zn = [dev(x, z - zlo + (zlo + i) % NZL, c, y) for i in range(1, NZL)]
    near = go([rcopy(wn_s, wn_r.at[i], n_ss.at[0, i], n_rs.at[0, i], d) for i, d in enumerate(zn)])
    arrive(pb)
    bias = b1[...]
    for i in range(NYX - 1):
        bias = bias + bp[i]
    bn_s[...] = bias
    nearb = go([rcopy(bn_s, bn_r.at[i], n_ss.at[1, i], n_rs.at[1, i], d) for i, d in enumerate(zn)])
    arrive(ph)
    hub = hub1[yx].astype(F32)
    for i in range(NYX - 1):
        hub = hub + hubp[i].astype(F32)
    for i in range(NZ):
        hz_s[i] = hub[2 * i:2 * i + 2, :]
    zh = go([rcopy(hz_s.at[k], hz_r.at[j], q_ss.at[j], q_rs.at[j], d)
             for j, (k, d) in enumerate(zp)])
    arrive(near)
    for i in range(NZL - 1):
        w = w + wn_r[i]
    wf_s[...] = w.astype(BF16)
    zf = [dev(x, (z + NZL * i) % NZ, c, y) for i in range(1, NZ // NZL)]
    farz = go([rcopy(wf_s, wf_r.at[i], f_ss.at[0, i], f_rs.at[0, i], d) for i, d in enumerate(zf)])
    arrive(nearb)
    for i in range(NZL - 1):
        bias = bias + bn_r[i]
    bf_s[...] = bias
    farb = go([rcopy(bf_s, bf_r.at[i], f_ss.at[1, i], f_rs.at[1, i], d) for i, d in enumerate(zf)])
    bwd.turn_b(0, NZ - 1)
    bwd.turn_a()
    fwd.sent()
    pl_all = div(lax.broadcasted_iota(jnp.int32, (1, halos), 1), 4)
    hot = hot_nodes(list_ids(send_ref, (mod(div(pl_all, NC), NX) * NZ + div(pl_all, NXC)) * NC
                             + mod(pl_all, NC)), rows)
    arrive(farz)
    w = wf_s[...].astype(F32)
    for i in range(NZ // NZL - 1):
        w = w + wf_r[i].astype(F32)
    wfull_ref[c, yx] = w.astype(BF16)
    ap = go([rcopy(wfull_ref.at[c, yx], wfull_ref.at[c, yx], ap_ss.at[i], ap_rs.at[i], d)
             for i, (k, d) in enumerate(yxp)])
    arrive(farb)
    for i in range(NZ // NZL - 1):
        bias = bias + bf_r[i]
    btot_ref[...] = bias
    flush_part(ch + pw + ph + pb + near + nearb + farz + farb + zh + cb + cw)
    arrive(zh)
    own = hz_s[z]
    for j in range(NZ - 1):
        own = own + hz_r[j]
    bwd.finish()
    total = base_v[...] + jnp.dot(hot, ret_ref[...].reshape(halos, width), preferred_element_type=F32)
    row = lax.broadcasted_iota(jnp.int32, (rows, 1), 0)
    for i in range(2):
        total = total + jnp.where(row == hub_ref[i], own[i:i + 1, :], 0.0)
    grad_v[...] = total.astype(BF16)
    stores[1].start()
    ac = pass_on(ap, wfull_ref, ac_ss, ac_rs)
    arrive(ac)
    flush()
    bwd.sent()
    for cp in stores:
        cp.wait()


def final_kernel(outs_hbm, grad_hbm, btot_hbm, wfull_hbm,
                 out_hbm, gout_hbm, us_hbm, un_hbm, ub_hbm, ov, gv, bv, wv, us, un, ub, sem, rsem):
    width = bv.shape[1]
    loads = [pltpu.make_async_copy(a, b, sem.at[i]) for i, (a, b) in enumerate(
        ((wfull_hbm, wv), (btot_hbm, bv), (outs_hbm, ov), (grad_hbm, gv)))]
    stores = [pltpu.make_async_copy(a, b, rsem.at[i]) for i, (a, b) in enumerate(
        ((us, us_hbm), (un, un_hbm), (ub, ub_hbm), (ov, out_hbm), (gv, gout_hbm)))]
    for cp in loads:
        cp.start()
    loads[0].wait()
    w = wv[...].reshape(2 * width, width).astype(F32)
    for o, ref in ((0, us), (width, un)):
        part = w[o:o + width, :]
        ref[...] = part * lax.rsqrt(jnp.mean(part * part) + UNIT_EPS)
    loads[1].wait()
    bias = bv[...]
    ub[...] = bias * lax.rsqrt(jnp.mean(bias * bias) + UNIT_EPS)
    for st in stores[:3]:
        st.start()
    for cp, st in zip(loads[2:], stores[3:]):
        cp.wait()
        st.start()
    for st in stores:
        st.wait()


def vmem():
    return pl.BlockSpec(memory_space=pltpu.VMEM)


def sds(shape, dtype):
    return jax.ShapeDtypeStruct(shape, dtype)


LIMIT = 56 << 20


def on_device(feats, w_self, w_neigh, bias, out_cot, degree, edge_src, hub_rows, send_rows):
    rows, width = feats.shape
    hubs = 2 * NC * NYX * NZ
    halos = 4 * NXC * NZ
    slots = rows + hubs + halos
    fan = edge_src.shape[1]
    wrows = 2 * width // (NC * NYX)
    dma = pltpu.SemaphoreType.DMA
    smem = pl.BlockSpec(memory_space=pltpu.SMEM)
    hbm = pl.BlockSpec(memory_space=pl.ANY)

    def vb(*shape):
        return pltpu.VMEM(shape, BF16)

    def vf(*shape):
        return pltpu.VMEM(shape, F32)

    send_t = send_rows.T
    outputs, grad, btot, wfull = pl.pallas_call(
        layer_kernel,
        out_shape=(sds((rows, width), BF16), sds((rows, width), BF16), sds((1, width), F32),
                   sds((NC, NYX, wrows, width), BF16)),
        in_specs=[hbm] * 4 + [vmem()] * 4 + [smem], out_specs=(hbm,) * 2 + (vmem(),) * 2,
        scratch_shapes=[
            vb(rows, width), vb(width, width), vb(width, width), vb(rows, width),
            pltpu.VMEM((fan, rows), jnp.int32), vb(slots, rows),
            vf(2, width), vf(NZ, 2, width), vf(2 * NZ, width), vb(NC, NYX, 2 * NZ, width),
            vb(NZ, NXC, 4, width), vf(width, rows), vf(rows, width), vf(rows, width),
            vb(width, rows), vb(rows, width), vb(rows, width), vb(width, rows),
            vb(rows, width), vf(rows, width), vb(rows, width), vb(NZ, NXC, 4, width),
            *[vb(NZ, NX, 4, width), vb(NX, NZ, 4, width), vb(NZ, NX, 4, width),
              vb(NZ, NXC, 4, width)] * 2,
            vb(NC, NYX, 2 * NZ, width), vf(NC, NYX, wrows, width), vf(1, width),
            vb(NYX, 2 * NZ, width), vf(NYX, wrows, width), vf(1, width),
            vb(NYX, 2 * NZ, width), vb(NYX, wrows, width), vf(1, width),
            vb(NYX - 1, 2 * NZ, width), vb(NYX - 1, wrows, width), vf(NYX - 1, 1, width),
            vf(wrows, width), vf(NZL - 1, wrows, width),
            vb(wrows, width), vb(max(NZ // NZL - 1, 1), wrows, width),
            vf(1, width), vf(NZL - 1, 1, width), vf(1, width), vf(max(NZ // NZL - 1, 1), 1, width),
            vf(NZ, 2, width), vf(NZ - 1, 2, width),
            dma((7,)), dma((NZ - 1,)), dma((NZ - 1,)), dma((NYX - 1,)), dma((NYX - 1,)),
            dma((NYX,)), dma((NYX,)),
            dma((3,)), dma((3,)), dma((3, NYX - 1)), dma((3, NYX - 1)), dma((NZ - 1,)), dma((NZ - 1,)),
            dma((2, NZL - 1)), dma((2, NZL - 1)),
            dma((2, max(NZ // NZL - 1, 1))), dma((2, max(NZ // NZL - 1, 1))),
            dma((NYX - 1,)), dma((NYX - 1,)), dma((NYX,)), dma((NYX,)),
            *[dma((4,)), dma((NZ - 1,)), dma((NZ - 1,)), dma((NX,)), dma((NXC,)),
              dma((NZ - 1,)), dma((NZ - 1,)), dma((NX,)), dma((NXC,))] * 2],
        compiler_params=pltpu.CompilerParams(
            collective_id=0, has_side_effects=True, vmem_limit_bytes=LIMIT),
    )(feats, w_self, w_neigh, out_cot, bias.reshape(1, width), degree.reshape(1, rows), edge_src.T,
      send_t, hub_rows)

    outputs, grad, us, un, ub = pl.pallas_call(
        final_kernel,
        out_shape=(sds((rows, width), BF16), sds((rows, width), BF16), sds((width, width), F32),
                   sds((width, width), F32), sds((1, width), F32)),
        in_specs=[hbm] * 4, out_specs=(hbm,) * 5,
        scratch_shapes=[vb(rows, width), vb(rows, width), vf(1, width), vb(NC, NYX, wrows, width),
                        vf(width, width), vf(width, width), vf(1, width), dma((4,)), dma((5,))],
        compiler_params=pltpu.CompilerParams(vmem_limit_bytes=LIMIT),
    )(outputs, grad, btot, wfull)
    return outputs, grad, us, un, ub.reshape(width)


def solution(mesh):
    both = ("dom", "rep")
    placed = (P(both, None), P(), P(), P(), P(both, None), P(both), P(both, None), P(both),
              P(both, None))
    return jax.shard_map(
        on_device,
        mesh=mesh,
        in_specs=placed,
        out_specs=(P(both, None), P(both, None), P(), P(), P()),
        check_vma=False,
    )
```

time: 76.5 us -> 73.7 us (0.963)
  Pallas kernels: 74.9 us -> 72.7 us
  local copies, waits for them, and re-layouts: 0.8 us -> 0 us
    pallas_call x1, Pallas kernels: 71.3 us -> 70.2 us  [on_device(): pl.pallas_call(layer_kernel, out_shape=(sds((rows, width), BF16), sds((ro...]
    pallas_call x1, Pallas kernels: 3.53 us -> 2.47 us  [on_device(): pl.pallas_call(final_kernel, out_shape=(sds((rows, width), BF16), sds((ro...]
    unnamed x3 -> x0, local copies, waits for them, and re-layouts: 0.8 us -> none
where the time goes in v3:
time: 73.7 us; the launch traced here: 73.5 us
  Pallas kernels  72.7 us (99%)
  between operations  0.8 us (1%)
    pallas_call x1, Pallas kernels, on_device(): pl.pallas_call(layer_kernel, out_shape=(sds((rows, width), BF16), sds((ro...  70.2 us
    pallas_call x1, Pallas kernels, on_device(): pl.pallas_call(final_kernel, out_shape=(sds((rows, width), BF16), sds((ro...  2.47 us

profile of v3, /device:TPU:1, one launch (start us, length us, event | category | flops | bytes accessed | tf_op | source)
XLA Modules:
  0.0 73.5 jit_solution(17669298679635754884)
XLA Ops:
  0.6 70.2 %shard_map.128 = (bf16[1024,256]{1,0:T(8,128)(2,1)}, bf16[1024,256]{1,0:T(8,128)(2,1)}, f32[1,256]{1,0:T(1,128)}, bf16[2,16,16,256]{3,2,1,0:T(8,128)(2,1)}) custom-call(bf16[1024,256]{1,0:T(8,128)(2,1)} %feats_hbm.1, bf16[256,256]{1,0:T(8,128)(2,1)} %ws_hbm.1, bf16[256,256]{1,0:T(8,128)(2,1)} %wn_hbm.1, bf16[1024,256]{1,0:T(8,128)(2,1)} %cot_hbm.1, ...), custom_call_target="tpu_custom_call" | custom-call | tf_op jit(solution)/shard_map/pallas_call | solution.py:520
  70.8 2.5 %shard_map.129 = (bf16[1024,256]{1,0:T(8,128)(2,1)}, bf16[1024,256]{1,0:T(8,128)(2,1)}, f32[256,256]{1,0:T(8,128)}, f32[256,256]{1,0:T(8,128)}, f32[1,256]{1,0:T(1,128)}) custom-call(bf16[1024,256]{1,0:T(8,128)(2,1)} %get-tuple-element.14.outs_hbm, bf16[1024,256]{1,0:T(8,128)(2,1)} %get-tuple-element.15.grad_hbm, f32[1,256]{1,0:T(1,128)} %get-tuple-element.16.btot_hbm, ...), custom_call_target="tpu_custom_call" | custom-call | tf_op jit(solution)/shard_map/pallas_call | solution.py:555

commit v4 on v3

--- a/solution.py
+++ b/solution.py
@@ -368,7 +368,6 @@
         egv[rs, :] = (lax.dot_general(glv[rs, :], wnv[...], NT, preferred_element_type=F32)
                       * dvs[rs, :]).astype(BF16)
     eg = egv[...]
-    flush_part(hz + hp + hc)
 
     hub_grad = jnp.dot(at[rows:rows + hubs, :], eg, preferred_element_type=F32)
     hubg[...] = hub_grad.reshape(hubg.shape).astype(BF16)
@@ -431,6 +430,7 @@
     pl_all = div(lax.broadcasted_iota(jnp.int32, (1, halos), 1), 4)
     hot = hot_nodes(list_ids(send_ref, (mod(div(pl_all, NC), NX) * NZ + div(pl_all, NXC)) * NC
                              + mod(pl_all, NC)), rows)
+    flush_part(hz + hp + hc + cw + cb + ch + pw + ph + pb + near + nearb)
     arrive(farz)
     w = wf_s[...].astype(F32)
     for i in range(NZ // NZL - 1):
@@ -442,7 +442,6 @@
     for i in range(NZ // NZL - 1):
         bias = bias + bf_r[i]
     btot_ref[...] = bias
-    flush_part(ch + pw + ph + pb + near + nearb + farz + farb + zh + cb + cw)
     arrive(zh)
     own = hz_s[z]
     for j in range(NZ - 1):

time: 73.7 us -> 73.5 us (level)
  no operation moved by 1% of the time
where the time goes in v4:
time: 73.5 us; the launch traced here: 73.3 us
  Pallas kernels  72.5 us (99%)
  between operations  0.8 us (1%)
    pallas_call x1, Pallas kernels, on_device(): pl.pallas_call(layer_kernel, out_shape=(sds((rows, width), BF16), sds((ro...  70 us
    pallas_call x1, Pallas kernels, on_device(): pl.pallas_call(final_kernel, out_shape=(sds((rows, width), BF16), sds((ro...  2.47 us

profile of v4, /device:TPU:1, one launch (start us, length us, event | category | flops | bytes accessed | tf_op | source)
XLA Modules:
  0.0 73.3 jit_solution(13192482303848332660)
XLA Ops:
  0.6 70.0 %shard_map.128 = (bf16[1024,256]{1,0:T(8,128)(2,1)}, bf16[1024,256]{1,0:T(8,128)(2,1)}, f32[1,256]{1,0:T(1,128)}, bf16[2,16,16,256]{3,2,1,0:T(8,128)(2,1)}) custom-call(bf16[1024,256]{1,0:T(8,128)(2,1)} %feats_hbm.1, bf16[256,256]{1,0:T(8,128)(2,1)} %ws_hbm.1, bf16[256,256]{1,0:T(8,128)(2,1)} %wn_hbm.1, bf16[1024,256]{1,0:T(8,128)(2,1)} %cot_hbm.1, ...), custom_call_target="tpu_custom_call" | custom-call | tf_op jit(solution)/shard_map/pallas_call | solution.py:519
  70.7 2.5 %shard_map.129 = (bf16[1024,256]{1,0:T(8,128)(2,1)}, bf16[1024,256]{1,0:T(8,128)(2,1)}, f32[256,256]{1,0:T(8,128)}, f32[256,256]{1,0:T(8,128)}, f32[1,256]{1,0:T(1,128)}) custom-call(bf16[1024,256]{1,0:T(8,128)(2,1)} %get-tuple-element.14.outs_hbm, bf16[1024,256]{1,0:T(8,128)(2,1)} %get-tuple-element.15.grad_hbm, f32[1,256]{1,0:T(1,128)} %get-tuple-element.16.btot_hbm, ...), custom_call_target="tpu_custom_call" | custom-call | tf_op jit(solution)/shard_map/pallas_call | solution.py:554
